TPU v7x, 32 devices: a whole 2x2x4 slice. The times are simulated.
32 devices in a mesh: tok: 8 (over z, core), rep: 4 (over y, x).
Axes of the slice: x: 2, y: 2, z: 4, core: 2. Of those that a mesh axis runs over, the one named last changes fastest.
Arguments:
- hidden_in: bfloat16 [4096, 4096], P('tok', 'rep'), may hold values from -9 to 9
- w_query: bfloat16 [4096, 4096], P(None, 'rep'), may hold values from -2 to 2
- w_key: bfloat16 [4096, 4096], P(None, 'rep'), may hold values from -2 to 2
- w_value: bfloat16 [4096, 4096], P(None, 'rep'), may hold values from -0.09375 to 0.09375
- w_out: bfloat16 [4096, 4096], P('rep'), may hold values from -3 to 3
- q_gain: float32 [4096], P('rep'), may hold values from 0.5 to 6
- k_gain: float32 [4096], P('rep'), may hold values from 0.5 to 6
- post_gain: float32 [4096], P('rep'), may hold values from 0.1 to 1.9
- prompt_lengths: int32 [8], replicated, may hold values from 1 to 2048, as said below
- segment_ids: int32 [4096], replicated, may hold values from 0 to 7, as said below
- deal: int32 [4096], replicated, may hold values from 0 to 4095, as said below
- inverse: int32 [4096], replicated, may hold values from 0 to 4095, as said below
- slots: int32 [4096], replicated, may hold values from 0 to 4095, as said below
Outputs:
- output: bfloat16 [4096, 4096], P('tok', 'rep')
- cache_keys: bfloat16 [4096, 4096], P('tok', 'rep')
- cache_values: bfloat16 [4096, 4096], P('tok', 'rep')
Inputs may be any that keep to these rules, and one draw needn't show every extreme that they name: `prompt_lengths`: the lengths sum to 4096; the longest prompt has exactly 2048 tokens. `segment_ids`: prompts lie in order: prompt s holds the prompt_lengths[s] packed tokens after those of prompts 0 to s - 1. `deal`: A permutation. For any two indices a and b of tok, exactly 64 of the packed tokens a * 512 to (a + 1) * 512 - 1 sit in dealt rows b * 512 to (b + 1) * 512 - 1. inverse[deal[q]] = q for every dealt row q. `slots`: A permutation. For any two indices a and b of tok, exactly 64 of the dealt rows a * 512 to (a + 1) * 512 - 1 have cache rows b * 512 to (b + 1) * 512 - 1.
All inputs are finite; a program needn't handle non-finite values.
Results may differ from a plain program's by a relative error of at most 0.012.
Values may be sent and summed in bfloat16 or wider, within the bound.
A program may use at most 128 MiB of HBM per device.

v0:
```python
import math

import jax
import jax.numpy as jnp
from jax import lax
from jax.sharding import PartitionSpec as P

HEAD_DIM = 128


EPSILON = 1e-06
ROPE_BASE = 500000.0


def rotate(values, positions):
    half_size = values.shape[-1] // 2
    frequency = ROPE_BASE ** (-jnp.arange(half_size, dtype=jnp.float32) * 2.0 / values.shape[-1])
    angles = positions.astype(jnp.float32)[:, None] * frequency[None, :]
    cosine = jnp.cos(angles)[:, None, :]
    sine_part = jnp.sin(angles)[:, None, :]
    lower_half = values[..., :half_size]
    upper_half = values[..., half_size:]
    return jnp.concatenate(
        [
            lower_half * cosine - upper_half * sine_part,
            upper_half * cosine + lower_half * sine_part,
        ],
        axis=-1,
    )


def bucketed(table_rows, row_order, shards):
    picked = table_rows[row_order]
    return picked.reshape(shards, picked.shape[0] // shards, picked.shape[1])


def placement_order(sources, shard_rows):
    local_ids = jnp.arange(sources.shape[0], dtype=jnp.int32)
    arrival = jnp.argsort(sources * shard_rows + local_ids)
    return jnp.argsort(arrival)


def body(
    hidden_in,
    w_query,
    w_key,
    w_value,
    w_out,
    q_gain,
    k_gain,
    post_gain,
    prompt_lengths,
    segment_ids,
    deal,
    inverse,
    slots,
):
    tok_rows, width_dev = hidden_in.shape
    full_width = w_query.shape[0]
    head_size = HEAD_DIM
    heads_dev = width_dev // head_size
    shards = lax.axis_size("tok")
    first_row = lax.axis_index("tok") * tok_rows
    my_packed = lax.dynamic_slice_in_dim(deal, first_row, tok_rows)
    my_segment = segment_ids[my_packed]
    prompt_ids = jnp.arange(prompt_lengths.shape[0], dtype=jnp.int32)
    prompt_starts = jnp.cumsum(prompt_lengths) - prompt_lengths
    my_start = jnp.sum(
        jnp.where(my_segment[:, None] == prompt_ids[None, :], prompt_starts[None, :], 0), axis=1
    )
    positions = my_packed - my_start
    pieces = lax.all_gather(hidden_in, "rep", axis=1, tiled=True)
    query_rows = jnp.dot(pieces, w_query, preferred_element_type=jnp.float32)
    key_rows = jnp.dot(pieces, w_key, preferred_element_type=jnp.float32)
    value_rows = jnp.dot(pieces, w_value, preferred_element_type=jnp.float32)
    query_sums, key_sums = lax.psum(
        (jnp.sum(query_rows * query_rows, axis=1), jnp.sum(key_rows * key_rows, axis=1)), "rep"
    )
    query_rows = (
        query_rows * lax.rsqrt(query_sums / full_width + EPSILON)[:, None] * q_gain[None, :]
    )
    key_rows = key_rows * lax.rsqrt(key_sums / full_width + EPSILON)[:, None] * k_gain[None, :]
    query_rot = rotate(query_rows.reshape(tok_rows, heads_dev, head_size), positions).astype(
        jnp.bfloat16
    )
    key_rot = (
        rotate(key_rows.reshape(tok_rows, heads_dev, head_size), positions)
        .astype(jnp.bfloat16)
        .reshape(tok_rows, width_dev)
    )
    value_half = value_rows.astype(jnp.bfloat16)
    scale = head_size ** (-0.5)

    def attend(state_now, key_block, value_block, key_packed):
        row_top, totals, weighted = state_now
        block_keys = key_block.reshape(key_block.shape[0], heads_dev, head_size)
        block_values = value_block.reshape(value_block.shape[0], heads_dev, head_size)
        key_segment = segment_ids[key_packed]
        allowed = (key_segment[None, :] == my_segment[:, None]) & (
            key_packed[None, :] <= my_packed[:, None]
        )
        scores = (
            jnp.einsum("qhd,khd->hqk", query_rot, block_keys, preferred_element_type=jnp.float32)
            * scale
        )
        masked = jnp.where(allowed[None], scores, -1e30)
        new_top = jnp.maximum(row_top, jnp.max(masked, axis=2))
        weights = jnp.where(allowed[None], jnp.exp(masked - new_top[:, :, None]), 0.0)
        factor = jnp.exp(row_top - new_top)
        totals = totals * factor + jnp.sum(weights, axis=2)
        weighted = weighted * factor[:, :, None] + jnp.einsum(
            "hqk,khd->hqd",
            weights.astype(jnp.bfloat16),
            block_values,
            preferred_element_type=jnp.float32,
        )
        return (new_top, totals, weighted)

    start_state = (
        jnp.full((heads_dev, tok_rows), -1e30, jnp.float32),
        jnp.zeros((heads_dev, tok_rows), jnp.float32),
        jnp.zeros((heads_dev, tok_rows, head_size), jnp.float32),
    )
    owned_rows = lax.dynamic_slice_in_dim(jnp.argsort(slots), first_row, tok_rows)
    my_slots = lax.dynamic_slice_in_dim(slots, first_row, tok_rows)
    slot_order = jnp.argsort(my_slots)
    sent_keys, sent_values = (
        lax.all_to_all(
            bucketed(key_rot, slot_order, shards), "tok", split_axis=0, concat_axis=0, tiled=True
        ),
        lax.all_to_all(
            bucketed(value_half, slot_order, shards), "tok", split_axis=0, concat_axis=0, tiled=True
        ),
    )
    arrival = placement_order(owned_rows // tok_rows, tok_rows)
    cache_keys = sent_keys.reshape(tok_rows, width_dev)[arrival]
    cache_values = sent_values.reshape(tok_rows, width_dev)[arrival]
    pieces = (
        lax.all_gather(key_rot, "tok", axis=0, tiled=True),
        lax.all_gather(value_half, "tok", axis=0, tiled=True),
    )
    key_all = pieces[0]
    block_size = math.gcd(key_all.shape[0], tok_rows)
    block_count = key_all.shape[0] // block_size

    def advance(state_in, block_set):
        return (attend(state_in, block_set[0], block_set[1], block_set[2]), None)

    state_out, _ = lax.scan(
        advance,
        start_state,
        (
            key_all.reshape(block_count, block_size, width_dev),
            pieces[1].reshape(block_count, block_size, width_dev),
            deal.reshape(block_count, block_size),
        ),
    )
    row_top, totals, weighted = state_out
    attended = (
        (weighted / totals[:, :, None])
        .transpose(1, 0, 2)
        .reshape(tok_rows, width_dev)
        .astype(jnp.bfloat16)
    )
    mixed_rows = (
        lax.psum_scatter(
            lax.dot_general(
                w_out, attended, (((0,), (1,)), ((), ())), preferred_element_type=jnp.float32
            ).astype(jnp.bfloat16),
            "rep",
            scatter_dimension=0,
            tiled=True,
        )
        .astype(jnp.float32)
        .T
    )
    mixed_sums = lax.psum(jnp.sum(mixed_rows * mixed_rows, axis=1), "rep")
    normed_rows = (
        mixed_rows * lax.rsqrt(mixed_sums / full_width + EPSILON)[:, None] * post_gain[None, :]
    )
    result_rows = (hidden_in.astype(jnp.float32) + normed_rows).astype(jnp.bfloat16)
    packed_order = jnp.argsort(my_packed)
    returned = lax.all_to_all(
        bucketed(result_rows, packed_order, shards), "tok", split_axis=0, concat_axis=0, tiled=True
    )
    my_dealt = lax.dynamic_slice_in_dim(inverse, first_row, tok_rows)
    output = returned.reshape(tok_rows, width_dev)[placement_order(my_dealt // tok_rows, tok_rows)]
    return (output, cache_keys, cache_values)


def solution(mesh):
    return jax.shard_map(
        body,
        mesh=mesh,
        in_specs=(
            P("tok", "rep"),
            P(None, "rep"),
            P(None, "rep"),
            P(None, "rep"),
            P("rep", None),
            P("rep"),
            P("rep"),
            P("rep"),
            P(),
            P(),
            P(),
            P(),
            P(),
        ),
        out_specs=(P("tok", "rep"), P("tok", "rep"), P("tok", "rep")),
        check_vma=False,
    )
```

profile of v0, /device:TPU:0, one launch (start us, length us, event | category | flops | bytes accessed | tf_op | source)
XLA Modules:
  0.0 586.3 jit_solution(2845161934136654388)
XLA Ops:
  9.6 3.1 gather_fusion.1
  13.8 51.3 %all-gather.4.cloned.1.call-done = bf16[512,4096]{1,0:T(8,128)(2,1)} async-done(((bf16[512,1024]{1,0:T(8,128)(2,1)}), bf16[512,4096]{1,0:T(8,128)(2,1)}) %all-gather.4.cloned.1.call-update) | async-done | bytes 4194320 | tf_op jit(solution)/shard_map/all_gather | solution.py:72
  65.2 10.6 %multiply_reduce_fusion.1 = (f32[512]{0:T(512)S(1)}, f32[512,1024]{1,0:T(8,128)}) fusion(bf16[512,4096]{1,0:T(8,128)(2,1)} %all-gather.4.cloned.1.call-done, bf16[4096,1024]{1,0:T(8,128)(2,1)} %param.17), kind=kOutput, calls=%fused_computation.47 | convolution fusion | flops 4296015360 | bytes 14682112 | tf_op jit(solution)/shard_map/dot_general | solution.py:74
  75.8 7.0 %multiply_reduce_fusion = (f32[512]{0:T(512)S(1)}, f32[512,1024]{1,0:T(8,128)S(1)}) fusion(bf16[512,4096]{1,0:T(8,128)(2,1)S(1)} %copy-done.8, bf16[4096,1024]{1,0:T(8,128)(2,1)} %param.16), kind=kOutput, calls=%fused_computation.43 | convolution fusion | flops 4296015360 | bytes 14682112 | tf_op jit(solution)/shard_map/dot_general | solution.py:73
  82.8 8.9 %all-reduce = (f32[512]{0:T(512)S(1)}, f32[512]{0:T(512)S(1)}) all-reduce(f32[512]{0:T(512)S(1)} %get-tuple-element.181, f32[512]{0:T(512)S(1)} %get-tuple-element.183), channel_id=1, replica_groups=mesh['tok'=8,'rep'=4] {'rep'}, use_global_device_ids=true, to_apply=%region_1.2 | all-reduce | flops 1024 | bytes 8192 | tf_op jit(solution)/shard_map/psum | solution.py:76
  99.6 10.1 %convolution_convert_fusion.1 = bf16[512,1024]{1,0:T(8,128)(2,1)} fusion(bf16[512,4096]{1,0:T(8,128)(2,1)} %all-gather.4.cloned.1.call-done, bf16[4096,1024]{1,0:T(8,128)(2,1)} %param.18), kind=kOutput, calls=%fused_computation.48 | convolution fusion | flops 4295491584 | bytes 13631488 | tf_op jit(solution)/shard_map/dot_general | solution.py:75
  111.4 70.1 %all-gather.6.cloned.1.call-done = bf16[4096,1024]{1,0:T(8,128)(2,1)} async-done(((bf16[512,1024]{1,0:T(8,128)(2,1)}), bf16[4096,1024]{1,0:T(8,128)(2,1)}) %all-gather.6.cloned.1.call-update) | async-done | bytes 8388624 | tf_op jit(solution)/shard_map/all_gather | solution.py:139
  181.6 82.7 %all-gather.8.cloned.1.call-done = bf16[4096,1024]{1,0:T(8,128)(2,1)} async-done(((bf16[512,1024]{1,0:T(8,128)(2,1)}), bf16[4096,1024]{1,0:T(8,128)(2,1)}) %all-gather.8.cloned.1.call-update) | async-done | bytes 8388624 | tf_op jit(solution)/shard_map/all_gather | solution.py:140
  264.3 202.6 %while.15 = (s32[]{:T(128)}, f32[8,512]{1,0:T(8,128)S(1)}, f32[8,512]{1,0:T(8,128)S(1)}, f32[8,512,128]{2,1,0:T(8,128)}, s32[8,512]{1,0:T(8,128)S(1)}, /*index=5...) while((s32[]{:T(128)}, f32[8,512]{1,0:T(8,128)S(1)}, ...), condition=%wide.region_9.10_spmd.clone, body=%wide.region_6.9_spmd.clone.sunk | while | flops 1103387136 | bytes 42231948 | solution.py:149
  270.0 6.1 %fusion.52 = (f32[8,512]{1,0:T(8,128)S(1)}, f32[8,512,512]{2,1,0:T(8,128)}) fusion(pred[512,512]{0,1:T(8,128)(4,1)S(1)} %compare_and_fusion.2, bf16[512,8,128]{0,2,1:T(8,128)(2,1)S(1)} %bitcast.85, bf16[512,8,128]{2,0,1:T(8,128)(2,1)} %get-tuple-element.307), kind=kOutput, calls=%fused_computation.10.clone.1 | convolution fusion | flops 543158272 | bytes 10764288 | tf_op jit(solution)/shard_map/while/body/eval_jaxpr/qhd,khd->hqk/dot_general | solution.py:103
  276.2 4.5 fusion.53
  281.2 7.9 %fusion.55 = f32[8,512,128]{2,1,0:T(8,128)} fusion(f32[8,512,128]{2,1,0:T(8,128)} %get-tuple-element.288, bf16[512,8,128]{0,2,1:T(8,128)(2,1)S(1)} %bitcast.89, f32[8,512,512]{2,1,0:T(8,128)} %get-tuple-element.268, f32[8,512]{1,0:T(8,128)S(1)} %select_maximum_fusion.2, pred[512,512]{0,1:T(8,128)(4,1)S(1)} %compare_and_fusion.2, ...), kind=kOutput, calls=%fused_computation.16.clone.1 | convolution fusion | flops 548929536 | bytes 13926401 | tf_op jit(solution)/shard_map/while/body/eval_jaxpr/hqk,khd->hqd/dot_general | solution.py:111
  289.1 3.1 gather_fusion
  294.8 6.1 %fusion.52 = (f32[8,512]{1,0:T(8,128)S(1)}, f32[8,512,512]{2,1,0:T(8,128)}) fusion(pred[512,512]{0,1:T(8,128)(4,1)S(1)} %compare_and_fusion.2, bf16[512,8,128]{0,2,1:T(8,128)(2,1)S(1)} %bitcast.85, bf16[512,8,128]{2,0,1:T(8,128)(2,1)} %get-tuple-element.307), kind=kOutput, calls=%fused_computation.10.clone.1 | convolution fusion | flops 543158272 | bytes 10764288 | tf_op jit(solution)/shard_map/while/body/eval_jaxpr/qhd,khd->hqk/dot_general | solution.py:103
  301.0 4.5 fusion.53
  306.0 8.5 %fusion.55 = f32[8,512,128]{2,1,0:T(8,128)} fusion(f32[8,512,128]{2,1,0:T(8,128)} %get-tuple-element.288, bf16[512,8,128]{0,2,1:T(8,128)(2,1)S(1)} %bitcast.89, f32[8,512,512]{2,1,0:T(8,128)} %get-tuple-element.268, f32[8,512]{1,0:T(8,128)S(1)} %select_maximum_fusion.2, pred[512,512]{0,1:T(8,128)(4,1)S(1)} %compare_and_fusion.2, ...), kind=kOutput, calls=%fused_computation.16.clone.1 | convolution fusion | flops 548929536 | bytes 13926401 | tf_op jit(solution)/shard_map/while/body/eval_jaxpr/hqk,khd->hqd/dot_general | solution.py:111
  320.2 6.1 %fusion.52 = (f32[8,512]{1,0:T(8,128)S(1)}, f32[8,512,512]{2,1,0:T(8,128)}) fusion(pred[512,512]{0,1:T(8,128)(4,1)S(1)} %compare_and_fusion.2, bf16[512,8,128]{0,2,1:T(8,128)(2,1)S(1)} %bitcast.85, bf16[512,8,128]{2,0,1:T(8,128)(2,1)} %get-tuple-element.307), kind=kOutput, calls=%fused_computation.10.clone.1 | convolution fusion | flops 543158272 | bytes 10764288 | tf_op jit(solution)/shard_map/while/body/eval_jaxpr/qhd,khd->hqk/dot_general | solution.py:103
  326.4 4.5 fusion.53
  331.4 8.5 %fusion.55 = f32[8,512,128]{2,1,0:T(8,128)} fusion(f32[8,512,128]{2,1,0:T(8,128)} %get-tuple-element.288, bf16[512,8,128]{0,2,1:T(8,128)(2,1)S(1)} %bitcast.89, f32[8,512,512]{2,1,0:T(8,128)} %get-tuple-element.268, f32[8,512]{1,0:T(8,128)S(1)} %select_maximum_fusion.2, pred[512,512]{0,1:T(8,128)(4,1)S(1)} %compare_and_fusion.2, ...), kind=kOutput, calls=%fused_computation.16.clone.1 | convolution fusion | flops 548929536 | bytes 13926401 | tf_op jit(solution)/shard_map/while/body/eval_jaxpr/hqk,khd->hqd/dot_general | solution.py:111
  345.6 6.1 %fusion.52 = (f32[8,512]{1,0:T(8,128)S(1)}, f32[8,512,512]{2,1,0:T(8,128)}) fusion(pred[512,512]{0,1:T(8,128)(4,1)S(1)} %compare_and_fusion.2, bf16[512,8,128]{0,2,1:T(8,128)(2,1)S(1)} %bitcast.85, bf16[512,8,128]{2,0,1:T(8,128)(2,1)} %get-tuple-element.307), kind=kOutput, calls=%fused_computation.10.clone.1 | convolution fusion | flops 543158272 | bytes 10764288 | tf_op jit(solution)/shard_map/while/body/eval_jaxpr/qhd,khd->hqk/dot_general | solution.py:103
  351.8 4.5 fusion.53
  356.8 8.5 %fusion.55 = f32[8,512,128]{2,1,0:T(8,128)} fusion(f32[8,512,128]{2,1,0:T(8,128)} %get-tuple-element.288, bf16[512,8,128]{0,2,1:T(8,128)(2,1)S(1)} %bitcast.89, f32[8,512,512]{2,1,0:T(8,128)} %get-tuple-element.268, f32[8,512]{1,0:T(8,128)S(1)} %select_maximum_fusion.2, pred[512,512]{0,1:T(8,128)(4,1)S(1)} %compare_and_fusion.2, ...), kind=kOutput, calls=%fused_computation.16.clone.1 | convolution fusion | flops 548929536 | bytes 13926401 | tf_op jit(solution)/shard_map/while/body/eval_jaxpr/hqk,khd->hqd/dot_general | solution.py:111
  371.0 6.1 %fusion.52 = (f32[8,512]{1,0:T(8,128)S(1)}, f32[8,512,512]{2,1,0:T(8,128)}) fusion(pred[512,512]{0,1:T(8,128)(4,1)S(1)} %compare_and_fusion.2, bf16[512,8,128]{0,2,1:T(8,128)(2,1)S(1)} %bitcast.85, bf16[512,8,128]{2,0,1:T(8,128)(2,1)} %get-tuple-element.307), kind=kOutput, calls=%fused_computation.10.clone.1 | convolution fusion | flops 543158272 | bytes 10764288 | tf_op jit(solution)/shard_map/while/body/eval_jaxpr/qhd,khd->hqk/dot_general | solution.py:103
  377.2 4.5 fusion.53
  382.2 8.5 %fusion.55 = f32[8,512,128]{2,1,0:T(8,128)} fusion(f32[8,512,128]{2,1,0:T(8,128)} %get-tuple-element.288, bf16[512,8,128]{0,2,1:T(8,128)(2,1)S(1)} %bitcast.89, f32[8,512,512]{2,1,0:T(8,128)} %get-tuple-element.268, f32[8,512]{1,0:T(8,128)S(1)} %select_maximum_fusion.2, pred[512,512]{0,1:T(8,128)(4,1)S(1)} %compare_and_fusion.2, ...), kind=kOutput, calls=%fused_computation.16.clone.1 | convolution fusion | flops 548929536 | bytes 13926401 | tf_op jit(solution)/shard_map/while/body/eval_jaxpr/hqk,khd->hqd/dot_general | solution.py:111
  396.4 6.1 %fusion.52 = (f32[8,512]{1,0:T(8,128)S(1)}, f32[8,512,512]{2,1,0:T(8,128)}) fusion(pred[512,512]{0,1:T(8,128)(4,1)S(1)} %compare_and_fusion.2, bf16[512,8,128]{0,2,1:T(8,128)(2,1)S(1)} %bitcast.85, bf16[512,8,128]{2,0,1:T(8,128)(2,1)} %get-tuple-element.307), kind=kOutput, calls=%fused_computation.10.clone.1 | convolution fusion | flops 543158272 | bytes 10764288 | tf_op jit(solution)/shard_map/while/body/eval_jaxpr/qhd,khd->hqk/dot_general | solution.py:103
  402.5 4.5 fusion.53
  407.6 8.5 %fusion.55 = f32[8,512,128]{2,1,0:T(8,128)} fusion(f32[8,512,128]{2,1,0:T(8,128)} %get-tuple-element.288, bf16[512,8,128]{0,2,1:T(8,128)(2,1)S(1)} %bitcast.89, f32[8,512,512]{2,1,0:T(8,128)} %get-tuple-element.268, f32[8,512]{1,0:T(8,128)S(1)} %select_maximum_fusion.2, pred[512,512]{0,1:T(8,128)(4,1)S(1)} %compare_and_fusion.2, ...), kind=kOutput, calls=%fused_computation.16.clone.1 | convolution fusion | flops 548929536 | bytes 13926401 | tf_op jit(solution)/shard_map/while/body/eval_jaxpr/hqk,khd->hqd/dot_general | solution.py:111
  421.8 6.1 %fusion.52 = (f32[8,512]{1,0:T(8,128)S(1)}, f32[8,512,512]{2,1,0:T(8,128)}) fusion(pred[512,512]{0,1:T(8,128)(4,1)S(1)} %compare_and_fusion.2, bf16[512,8,128]{0,2,1:T(8,128)(2,1)S(1)} %bitcast.85, bf16[512,8,128]{2,0,1:T(8,128)(2,1)} %get-tuple-element.307), kind=kOutput, calls=%fused_computation.10.clone.1 | convolution fusion | flops 543158272 | bytes 10764288 | tf_op jit(solution)/shard_map/while/body/eval_jaxpr/qhd,khd->hqk/dot_general | solution.py:103
  427.9 4.5 fusion.53
  433.0 8.5 %fusion.55 = f32[8,512,128]{2,1,0:T(8,128)} fusion(f32[8,512,128]{2,1,0:T(8,128)} %get-tuple-element.288, bf16[512,8,128]{0,2,1:T(8,128)(2,1)S(1)} %bitcast.89, f32[8,512,512]{2,1,0:T(8,128)} %get-tuple-element.268, f32[8,512]{1,0:T(8,128)S(1)} %select_maximum_fusion.2, pred[512,512]{0,1:T(8,128)(4,1)S(1)} %compare_and_fusion.2, ...), kind=kOutput, calls=%fused_computation.16.clone.1 | convolution fusion | flops 548929536 | bytes 13926401 | tf_op jit(solution)/shard_map/while/body/eval_jaxpr/hqk,khd->hqd/dot_general | solution.py:111
  447.2 6.1 %fusion.52 = (f32[8,512]{1,0:T(8,128)S(1)}, f32[8,512,512]{2,1,0:T(8,128)}) fusion(pred[512,512]{0,1:T(8,128)(4,1)S(1)} %compare_and_fusion.2, bf16[512,8,128]{0,2,1:T(8,128)(2,1)S(1)} %bitcast.85, bf16[512,8,128]{2,0,1:T(8,128)(2,1)} %get-tuple-element.307), kind=kOutput, calls=%fused_computation.10.clone.1 | convolution fusion | flops 543158272 | bytes 10764288 | tf_op jit(solution)/shard_map/while/body/eval_jaxpr/qhd,khd->hqk/dot_general | solution.py:103
  453.3 4.5 fusion.53
  458.4 8.5 %fusion.55 = f32[8,512,128]{2,1,0:T(8,128)} fusion(f32[8,512,128]{2,1,0:T(8,128)} %get-tuple-element.288, bf16[512,8,128]{0,2,1:T(8,128)(2,1)S(1)} %bitcast.89, f32[8,512,512]{2,1,0:T(8,128)} %get-tuple-element.268, f32[8,512]{1,0:T(8,128)S(1)} %select_maximum_fusion.2, pred[512,512]{0,1:T(8,128)(4,1)S(1)} %compare_and_fusion.2, ...), kind=kOutput, calls=%fused_computation.16.clone.1 | convolution fusion | flops 548929536 | bytes 13926401 | tf_op jit(solution)/shard_map/while/body/eval_jaxpr/hqk,khd->hqd/dot_general | solution.py:111
  469.1 9.5 %fusion.13 = bf16[4096,512]{0,1:T(8,128)(2,1)} fusion(bf16[512,1024]{0,1:T(8,128)(2,1)S(1)} %bitcast.95, bf16[1024,4096]{1,0:T(8,128)(2,1)} %param.19), kind=kOutput, calls=%fused_computation.31 | convolution fusion | flops 4297064448 | bytes 13631488 | tf_op jit(solution)/shard_map/dot_general | solution.py:167
  479.4 3.8 sort.107
  485.9 3.9 all-to-all-start.1
  492.6 23.5 %all-to-all-done.1 = bf16[8,64,1024]{2,1,0:T(8,128)(2,1)S(1)} async-done(((bf16[8,64,1024]{2,1,0:T(8,128)(2,1)}), bf16[8,64,1024]{2,1,0:T(8,128)(2,1)S(1)}, u32[]{:S(2)}, u32[]{:S(2)}) %all-to-all-start.1) | async-done | bytes 1048608 | tf_op jit(solution)/shard_map/all_to_all | solution.py:128
  516.1 3.6 all-to-all-start.2
  519.7 3.8 sort.104
  523.5 6.4 %reduce-scatter.2.cloned.1.call-done = bf16[1024,512]{0,1:T(8,128)(2,1)} async-done(((bf16[4096,512]{0,1:T(8,128)(2,1)}), bf16[1024,512]{0,1:T(8,128)(2,1)}) %reduce-scatter.2.cloned.1.call-update) | async-done | bytes 1048592 | tf_op jit(solution)/shard_map/reduce_scatter | solution.py:166
  531.4 8.9 %psum.23 = f32[512]{0:T(512)S(1)} all-reduce(f32[512]{0:T(512)S(1)} %fusion.14), channel_id=1, replica_groups=mesh['tok'=8,'rep'=4] {'rep'}, use_global_device_ids=true, to_apply=%region_12.13 | all-reduce | flops 512 | bytes 4096 | tf_op jit(solution)/shard_map/psum | solution.py:177
  546.2 3.6 all-to-all-start
  549.8 5.8 sort.108
  556.3 3.8 sort.105
  560.1 3.8 sort.106
  563.9 3.8 sort.109
  567.6 3.8 sort.110
  (159 shorter events, 84.8 us)
Async XLA Ops:
  7.2 5.6 copy-start.9
  7.2 2.4 copy-start
  7.2 58.0 %all-gather.4.cloned.1.call-start = ((), (), s32[]{:S(2)}) async-start(), calls=%async_computation.4 | async-start | bytes 5242880 | tf_op jit(solution)/shard_map/all_gather | solution.py:72
  7.9 173.7 %all-gather.6.cloned.1.call-start = ((), (), s32[]{:S(2)}) async-start(), calls=%async_computation.5 | async-start | bytes 9437184 | tf_op jit(solution)/shard_map/all_gather | solution.py:139
  65.2 10.6 %copy-start.8 = (bf16[512,4096]{1,0:T(8,128)(2,1)S(1)}, bf16[512,4096]{1,0:T(8,128)(2,1)}, u32[]{:S(2)}) copy-start(bf16[512,4096]{1,0:T(8,128)(2,1)} %all-gather.4.cloned.1.call-done) | copy-start | bytes 12582916
  75.8 16.0 %copy-start.5 = (f32[1024]{0:T(1024)S(1)}, f32[1024]{0:T(1024)}, u32[]{:S(2)}) copy-start(f32[1024]{0:T(1024)} %param.21) | copy-start | bytes 12292
  94.1 0.7 copy-start.6
  99.4 10.5 %copy-start.3 = (s32[4096]{0:T(1024)S(1)}, s32[4096]{0:T(1024)}, u32[]{:S(2)}) copy-start(s32[4096]{0:T(1024)} %param.25) | copy-start | bytes 49156
  99.4 164.9 %all-gather.8.cloned.1.call-start = ((), (), s32[]{:S(2)}) async-start(), calls=%async_computation.6 | async-start | bytes 9437184 | tf_op jit(solution)/shard_map/all_gather | solution.py:140
  109.8 420.1 %reduce-scatter.2.cloned.1.call-start = ((), (), s32[]{:S(2)}) async-start(), calls=%async_computation.7 | async-start | bytes 5242880 | tf_op jit(solution)/shard_map/reduce_scatter | solution.py:166
  478.6 0.7 copy-start.4
  478.6 4.6 copy-start.1
  485.9 3.9 copy-start.2
  485.9 30.2 %all-to-all-start.1 = ((bf16[8,64,1024]{2,1,0:T(8,128)(2,1)}), bf16[8,64,1024]{2,1,0:T(8,128)(2,1)S(1)}, u32[]{:S(2)}, u32[]{:S(2)}) async-start(bf16[8,64,1024]{2,1,0:T(8,128)(2,1)} %bitcast.10), calls=%async_computation.2 | async-start | bytes 2097152 | tf_op jit(solution)/shard_map/all_to_all | solution.py:128
  492.6 47.7 %copy-start.7 = (f32[1024]{0:T(1024)S(1)}, f32[1024]{0:T(1024)}, u32[]{:S(2)}) copy-start(f32[1024]{0:T(1024)} %param.22) | copy-start | bytes 12292
  516.1 30.1 %all-to-all-start.2 = ((bf16[8,64,1024]{2,1,0:T(8,128)(2,1)}), bf16[8,64,1024]{2,1,0:T(8,128)(2,1)S(1)}, u32[]{:S(2)}, u32[]{:S(2)}) async-start(bf16[8,64,1024]{2,1,0:T(8,128)(2,1)} %bitcast.12), calls=%async_computation.3 | async-start | bytes 2097152 | tf_op jit(solution)/shard_map/all_to_all | solution.py:131
  546.2 30.8 %all-to-all-start = ((bf16[8,64,1024]{2,1,0:T(8,128)(2,1)}), bf16[8,64,1024]{2,1,0:T(8,128)(2,1)S(1)}, u32[]{:S(2)}, u32[]{:S(2)}) async-start(bf16[8,64,1024]{2,1,0:T(8,128)(2,1)} %bitcast.92), calls=%async_computation.1 | async-start | bytes 2097152 | tf_op jit(solution)/shard_map/all_to_all | solution.py:183
Sparse Core Ops, SparseCore 0:
  9.8 55.2 all-gather.3
  99.5 82.0 all-gather.5
  183.8 80.5 all-gather.7
  478.7 51.1 reduce-scatter.1
where the time goes:
time: 587 us; the launch traced here: 586 us
  waiting for transfers between devices  236 us (40%)
  matrix products  153 us (26%)
  other arithmetic  80.8 us (14%)
  local copies, waits for them, and re-layouts  72.4 us (12%)
  blocking collectives  17.9 us (3%)
  between operations  14.1 us (2%)
  starting transfers between devices  11.4 us (2%)
    all_gather x1, waiting for transfers between devices, body(): lax.all_gather(value_half, 'tok', axis=0, tiled=True)  82.7 us
    all_gather x1, waiting for transfers between devices, body(): lax.all_gather(key_rot, 'tok', axis=0, tiled=True)  70.1 us
    dot_general x8, matrix products, attend(): jnp.einsum('hqk,khd->hqd', weights.astype(jnp.bfloat16), block_values, pr...  67.1 us
    all_gather x1, waiting for transfers between devices, body(): pieces = lax.all_gather(hidden_in, 'rep', axis=1, tiled=True)  51.3 us
    dot_general x8, matrix products, attend(): jnp.einsum('qhd,khd->hqk', query_rot, block_keys, preferred_element_type=...  49 us
    reduce_sum x8, other arithmetic, attend(): totals = totals * factor + jnp.sum(weights, axis=2)  35.9 us
    gather x8, local copies, waits for them, and re-layouts, attend(): key_segment = segment_ids[key_packed]  25.1 us
    all_to_all x1, waiting for transfers between devices, body(): lax.all_to_all(bucketed(key_rot, slot_order, shards), 'tok', split_axis=0...  23.5 us
  transfers between devices with their start and end apart: 7, of which 6 were waited for; matrix products, arithmetic and copies ran while one was open for 11% of the time, Pallas kernels for 0%

commit v1 on v0

--- a/solution.py
+++ b/solution.py
@@ -1,8 +1,11 @@
+import functools
 import math
 
 import jax
 import jax.numpy as jnp
 from jax import lax
+from jax.experimental import pallas as pl
+from jax.experimental.pallas import tpu as pltpu
 from jax.sharding import PartitionSpec as P
 
 HEAD_DIM = 128
@@ -188,9 +191,256 @@
     return (output, cache_keys, cache_values)
 
 
+def select_rows(hits, rows):
+    return jnp.dot(
+        hits.astype(jnp.bfloat16), rows, preferred_element_type=jnp.float32
+    ).astype(jnp.bfloat16)
+
+
+def attend_kernel(starts_ref, target_ref, qk_ref, v_ref, out_ref, keys, values, *, size, head_size):
+    block = pl.program_id(0)
+    mine = pl.ds(pl.multiple_of(block * size, size), size)
+    row_iota = lax.broadcasted_iota(jnp.int32, (size, size), 0)
+    column_iota = lax.broadcasted_iota(jnp.int32, (size, size), 1)
+    hits = jnp.where(row_iota == target_ref[0], 1.0, 0.0).astype(jnp.bfloat16)
+    qk_rows = qk_ref[...].reshape(size, 2 * head_size)
+    v_rows = v_ref[...].reshape(size, head_size)
+    packed_qk = jnp.dot(hits, qk_rows, preferred_element_type=jnp.float32).astype(jnp.bfloat16)
+    packed_v = jnp.dot(hits, v_rows, preferred_element_type=jnp.float32).astype(jnp.bfloat16)
+    query = packed_qk[:, :head_size]
+    keys[mine, :] = packed_qk[:, head_size:]
+    values[mine, :] = packed_v
+    first = block * size
+    rows = first + lax.broadcasted_iota(jnp.int32, (size, 1), 0)
+    row_start = jnp.zeros((size, 1), jnp.int32)
+    low = jnp.int32(0)
+    for prompt in range(starts_ref.shape[0]):
+        start = starts_ref[prompt]
+        row_start = jnp.where(rows >= start, jnp.maximum(row_start, start), row_start)
+        low = jnp.where(first >= start, jnp.maximum(low, start), low)
+    scale = head_size ** (-0.5) * math.log2(math.e)
+
+    def scores_of(key_rows):
+        return lax.dot_general(
+            query, key_rows, (((1,), (1,)), ((), ())), preferred_element_type=jnp.float32
+        ) * scale
+
+    local_start = row_start - first
+    allowed = (column_iota >= local_start) & (column_iota <= row_iota)
+    scores = jnp.where(allowed, scores_of(packed_qk[:, head_size:]), -1e30)
+    top = jnp.max(scores, axis=1, keepdims=True)
+    weights = jnp.exp2(scores - top)
+    totals = jnp.sum(weights, axis=1, keepdims=True)
+    weighted = jnp.dot(
+        weights.astype(jnp.bfloat16), packed_v, preferred_element_type=jnp.float32
+    )
+
+    def earlier(step, state):
+        top, totals, weighted = state
+        base = pl.multiple_of((block - 1 - step) * size, size)
+        scores = scores_of(keys[pl.ds(base, size), :])
+        scores = jnp.where(column_iota >= row_start - base, scores, -1e30)
+        new_top = jnp.maximum(top, jnp.max(scores, axis=1, keepdims=True))
+        factor = jnp.exp2(top - new_top)
+        weights = jnp.exp2(scores - new_top)
+        totals = totals * factor + jnp.sum(weights, axis=1, keepdims=True)
+        weighted = weighted * factor + jnp.dot(
+            weights.astype(jnp.bfloat16),
+            values[pl.ds(base, size), :],
+            preferred_element_type=jnp.float32,
+        )
+        return (new_top, totals, weighted)
+
+    top, totals, weighted = lax.fori_loop(
+        0, block - low // size, earlier, (top, totals, weighted)
+    )
+    out_ref[...] = (weighted / totals).astype(jnp.bfloat16)
+
+
+def attend_head(starts, target, qk_rows, v_rows):
+    shards, tok_rows, head_size = v_rows.shape
+    chunk = tok_rows // shards
+    return pl.pallas_call(
+        functools.partial(attend_kernel, size=tok_rows, head_size=head_size),
+        out_shape=jax.ShapeDtypeStruct((shards * tok_rows, head_size), jnp.bfloat16),
+        grid_spec=pltpu.PrefetchScalarGridSpec(
+            num_scalar_prefetch=1,
+            grid=(shards,),
+            in_specs=[
+                pl.BlockSpec((1, 1, tok_rows), lambda i, s: (i, 0, 0)),
+                pl.BlockSpec((shards, chunk, 2 * head_size), lambda i, s: (0, i, 0)),
+                pl.BlockSpec((shards, chunk, head_size), lambda i, s: (0, i, 0)),
+            ],
+            out_specs=pl.BlockSpec((tok_rows, head_size), lambda i, s: (i, 0)),
+            scratch_shapes=[
+                pltpu.VMEM((shards * tok_rows, head_size), jnp.bfloat16),
+                pltpu.VMEM((shards * tok_rows, head_size), jnp.bfloat16),
+            ],
+        ),
+        compiler_params=pltpu.CompilerParams(
+            dimension_semantics=("arbitrary",), vmem_limit_bytes=48 << 20
+        ),
+        cost_estimate=pl.CostEstimate(
+            flops=8 * tok_rows * tok_rows * shards * head_size * 3,
+            bytes_accessed=8 * shards * tok_rows * head_size,
+            transcendentals=3 * shards * tok_rows * tok_rows,
+        ),
+    )(starts, target, qk_rows, v_rows)
+
+
+def body_heads(
+    hidden_in,
+    w_query,
+    w_key,
+    w_value,
+    w_out,
+    q_gain,
+    k_gain,
+    post_gain,
+    prompt_lengths,
+    segment_ids,
+    deal,
+    inverse,
+    slots,
+):
+    tok_rows, width_dev = hidden_in.shape
+    full_width = w_query.shape[0]
+    head_size = HEAD_DIM
+    heads_dev = width_dev // head_size
+    shards = lax.axis_size("tok")
+    chunk = tok_rows // shards
+    me = lax.axis_index("tok")
+    first_row = me * tok_rows
+    pieces = lax.all_gather(hidden_in, "rep", axis=1, tiled=True)
+
+    local = jnp.arange(tok_rows, dtype=jnp.int32)
+    starts = jnp.cumsum(prompt_lengths) - prompt_lengths
+    my_packed = lax.dynamic_slice_in_dim(deal, first_row, tok_rows)
+    my_slots = lax.dynamic_slice_in_dim(slots, first_row, tok_rows)
+    rank = jnp.sum((my_packed[None, :] < my_packed[:, None]).astype(jnp.int32), axis=1)
+    sort_hits = rank[None, :] == local[:, None]
+    sorted_packed = jnp.sum(jnp.where(sort_hits, my_packed[None, :], 0), axis=1)
+    sorted_slots = jnp.sum(jnp.where(sort_hits, my_slots[None, :], 0), axis=1)
+    my_start = jnp.max(
+        jnp.where(starts[None, :] <= sorted_packed[:, None], starts[None, :], 0), axis=1
+    )
+    positions = sorted_packed - my_start
+
+    source = inverse.reshape(shards, tok_rows) // tok_rows
+    before = (source[:, None, :] == source[:, :, None]) & (local[None, None, :] < local[None, :, None])
+    arrived = source * chunk + jnp.sum(before.astype(jnp.int32), axis=2)
+    target = jnp.sum(
+        jnp.where(arrived[:, :, None] == local[None, None, :], local[None, :, None], 0), axis=1
+    )
+
+    slot_rank = jnp.sum((sorted_slots[None, :] < sorted_slots[:, None]).astype(jnp.int32), axis=1)
+    slot_hits = slot_rank[None, :] == local[:, None]
+    slot_rows = slots.reshape(shards, tok_rows) - first_row
+    owned = (slot_rows >= 0) & (slot_rows < tok_rows)
+    ahead = owned[:, None, :] & (slot_rows[:, None, :] < slot_rows[:, :, None])
+    landed = jnp.arange(shards, dtype=jnp.int32)[:, None] * chunk + jnp.sum(
+        ahead.astype(jnp.int32), axis=2
+    )
+    landed = jnp.where(owned, landed, -1).reshape(-1)
+    slot_target = jnp.sum(
+        jnp.where(landed[:, None] == local[None, :], slot_rows.reshape(-1)[:, None], 0), axis=0
+    )
+
+    sent_hidden = lax.all_to_all(
+        select_rows(sort_hits, hidden_in).reshape(shards, chunk, width_dev),
+        "tok",
+        split_axis=0,
+        concat_axis=0,
+        tiled=True,
+    )
+    my_target = lax.dynamic_index_in_dim(target, me, 0, keepdims=False)
+    my_hits = my_target[None, :] == local[:, None]
+    packed_hidden = select_rows(my_hits, sent_hidden.reshape(tok_rows, width_dev))
+
+    pieces = select_rows(sort_hits, pieces)
+    query_rows = jnp.dot(pieces, w_query, preferred_element_type=jnp.float32)
+    key_rows = jnp.dot(pieces, w_key, preferred_element_type=jnp.float32)
+    sums = jnp.stack(
+        [jnp.sum(query_rows * query_rows, axis=1), jnp.sum(key_rows * key_rows, axis=1)]
+    )
+    sums = lax.psum(sums, "rep")
+    value_half = jnp.dot(pieces, w_value, preferred_element_type=jnp.float32).astype(jnp.bfloat16)
+    query_rows = query_rows * lax.rsqrt(sums[0] / full_width + EPSILON)[:, None] * q_gain[None, :]
+    key_rows = key_rows * lax.rsqrt(sums[1] / full_width + EPSILON)[:, None] * k_gain[None, :]
+    query_rot = rotate(query_rows.reshape(tok_rows, heads_dev, head_size), positions).astype(
+        jnp.bfloat16
+    )
+    key_rot = rotate(key_rows.reshape(tok_rows, heads_dev, head_size), positions).astype(
+        jnp.bfloat16
+    )
+    v_rows = lax.all_to_all(
+        value_half.reshape(tok_rows, heads_dev, head_size).transpose(1, 0, 2),
+        "tok",
+        split_axis=0,
+        concat_axis=0,
+        tiled=True,
+    )
+    qk_rows = lax.all_to_all(
+        jnp.concatenate([query_rot, key_rot], axis=2).transpose(1, 0, 2),
+        "tok",
+        split_axis=0,
+        concat_axis=0,
+        tiled=True,
+    )
+    key_flat, value_half, qk_rows, v_rows = lax.optimization_barrier(
+        (key_rot.reshape(tok_rows, width_dev), value_half, qk_rows, v_rows)
+    )
+    sent_keys, sent_values = [
+        lax.all_to_all(
+            select_rows(slot_hits, rows).reshape(shards, chunk, width_dev),
+            "tok",
+            split_axis=0,
+            concat_axis=0,
+            tiled=True,
+        )
+        for rows in (key_flat, value_half)
+    ]
+    cache_hits = slot_target[None, :] == local[:, None]
+    cache_keys = select_rows(cache_hits, sent_keys.reshape(tok_rows, width_dev))
+    cache_values = select_rows(cache_hits, sent_values.reshape(tok_rows, width_dev))
+
+    attended = attend_head(starts, target[:, None, :], qk_rows, v_rows)
+    attended = lax.all_to_all(
+        attended.reshape(shards, tok_rows, head_size),
+        "tok",
+        split_axis=0,
+        concat_axis=0,
+        tiled=True,
+    )
+    attended = attended.transpose(1, 0, 2).reshape(tok_rows, width_dev)
+    mixed_rows = (
+        lax.psum_scatter(
+            lax.dot_general(
+                w_out, attended, (((0,), (1,)), ((), ())), preferred_element_type=jnp.float32
+            ).astype(jnp.bfloat16),
+            "rep",
+            scatter_dimension=0,
+            tiled=True,
+        )
+        .astype(jnp.float32)
+        .T
+    )
+    mixed_sums = lax.psum(jnp.sum(mixed_rows * mixed_rows, axis=1), "rep")
+    normed_rows = (
+        mixed_rows * lax.rsqrt(mixed_sums / full_width + EPSILON)[:, None] * post_gain[None, :]
+    )
+    output = (packed_hidden.astype(jnp.float32) + normed_rows).astype(jnp.bfloat16)
+    return (output, cache_keys, cache_values)
+
+
 def solution(mesh):
+    def pick(*operands):
+        heads_dev = operands[0].shape[1] // HEAD_DIM
+        chosen = body_heads if heads_dev == mesh.shape["tok"] else body
+        return chosen(*operands)
+
     return jax.shard_map(
-        body,
+        pick,
         mesh=mesh,
         in_specs=(
             P("tok", "rep"),

time: 587 us -> 359 us (0.61)
  matrix products: 153 us -> 46.1 us
  waiting for transfers between devices: 236 us -> 153 us
  other arithmetic: 80.8 us -> 24.4 us
  local copies, waits for them, and re-layouts: 72.4 us -> 32.3 us
  blocking collectives: 17.9 us -> 46.8 us
  Pallas kernels: 0 us -> 19.8 us
  starting transfers between devices: 11.4 us -> 21.1 us
    all_gather x3 -> x1, waiting for transfers between devices: 204 us -> 51.8 us  [body_heads(): pieces = lax.all_gather(hidden_in, 'rep', axis=1, tiled=True)]
    dot_general x20 -> x11, matrix products: 153 us -> 46.1 us  [the longest x7 16.1 us: select_rows(): jnp.dot(hits.astype(jnp.bfloat16), rows, preferred_element_type=jnp.float32)]
    all_to_all x3 -> x5, waiting for transfers between devices: 24.6 us -> 101 us  [the longest x2 47.8 us: body_heads(): lax.all_to_all(select_rows(slot_hits, rows).reshape(shards, chunk, width_...]
    gather x15 -> x0, local copies, waits for them, and re-layouts: 44.9 us -> none  [the longest x8 25.1 us: attend(): key_segment = segment_ids[key_packed]]
    all_to_all x0 -> x1, blocking collectives: none -> 29 us  [body_heads(): lax.all_to_all(attended.reshape(shards, tok_rows, head_size), 'tok', spli...]
    sort x7 -> x0, other arithmetic: 28.4 us -> none  [the longest x2 7.54 us: placement_order(): return jnp.argsort(arrival)]
    reduce_sum x10 -> x8, other arithmetic: 37.4 us -> 9.95 us  [the longest x1 2.39 us: body_heads(): jnp.sum(jnp.where(landed[:, None] == local[None, :], slot_rows.reshape(-1...]
    dynamic_slice x25 -> x3, local copies, waits for them, and re-layouts: 22.5 us -> 1.53 us  [the longest x1 0.76 us: body_heads(): my_packed = lax.dynamic_slice_in_dim(deal, first_row, tok_rows)]
  transfers between devices with their start and end apart: 7 -> 7, of which waited for: 6 -> 5; matrix products, arithmetic and copies ran while one was open for 11% -> 15% of each run, Pallas kernels for 0% -> 0%
where the time goes in v1:
time: 359 us; the launch traced here: 358 us
  waiting for transfers between devices  153 us (43%)
  blocking collectives  46.8 us (13%)
  matrix products  46.1 us (13%)
  local copies, waits for them, and re-layouts  32.3 us (9%)
  other arithmetic  24.4 us (7%)
  starting transfers between devices  21.1 us (6%)
  Pallas kernels  19.8 us (6%)
  between operations  14.4 us (4%)
    all_gather x1, waiting for transfers between devices, body_heads(): pieces = lax.all_gather(hidden_in, 'rep', axis=1, tiled=True)  51.8 us
    all_to_all x2, waiting for transfers between devices, body_heads(): lax.all_to_all(select_rows(slot_hits, rows).reshape(shards, chunk, width_...  47.8 us
    all_to_all x1, waiting for transfers between devices, body_heads(): lax.all_to_all(jnp.concatenate([query_rot, key_rot], axis=2).transpose(1,...  42.7 us
    all_to_all x1, blocking collectives, body_heads(): lax.all_to_all(attended.reshape(shards, tok_rows, head_size), 'tok', spli...  29 us
    pallas_call x1, Pallas kernels, attend_head(): pl.pallas_call(functools.partial(attend_kernel, size=tok_rows, head_size=...  19.8 us
    dot_general x7, matrix products, select_rows(): jnp.dot(hits.astype(jnp.bfloat16), rows, preferred_element_type=jnp.float32)  16.1 us
    unnamed x37, local copies, waits for them, and re-layouts  14.7 us
    dot_general x1, matrix products, body_heads(): jnp.dot(pieces, w_value, preferred_element_type=jnp.float32)  10.1 us
  transfers between devices with their start and end apart: 7, of which 5 were waited for; matrix products, arithmetic and copies ran while one was open for 15% of the time, Pallas kernels for 0%

profile of v1, /device:TPU:0, one launch (start us, length us, event | category | flops | bytes accessed | tf_op | source)
XLA Modules:
  0.0 357.9 jit_solution(8558855063402313504)
XLA Ops:
  11.6 1.7 multiply_cosine_fusion
  13.4 51.8 %all-gather.2.cloned.1.call-done = bf16[512,4096]{1,0:T(8,128)(2,1)} async-done(((bf16[512,1024]{1,0:T(8,128)(2,1)}), bf16[512,4096]{1,0:T(8,128)(2,1)}) %all-gather.2.cloned.1.call-update) | async-done | bytes 4194320 | tf_op jit(solution)/shard_map/all_gather | solution.py:314
  65.2 4.7 %convolution_convert_fusion.1 = bf16[512,4096]{1,0:T(8,128)(2,1)S(1)} fusion(bf16[512,4096]{1,0:T(8,128)(2,1)} %all-gather.2.cloned.1.call-done, s32[512]{0:T(512)S(1)} %convert_reduce_fusion.3), kind=kOutput, calls=%fused_computation.7 | convolution fusion | flops 2149842944 | bytes 8390656 | tf_op jit(solution)/shard_map/dot_general | solution.py:195
  69.9 4.6 %multiply_reduce_fusion.1 = (f32[512]{0:T(512)S(1)}, f32[512,1024]{1,0:T(8,128)S(1)}) fusion(bf16[512,4096]{1,0:T(8,128)(2,1)S(1)} %convolution_convert_fusion.1, bf16[4096,1024]{1,0:T(8,128)(2,1)S(1)} %copy-done.11), kind=kOutput, calls=%fused_computation.25 | convolution fusion | flops 4296015360 | bytes 14682112 | tf_op jit(solution)/shard_map/dot_general | solution.py:361
  74.5 5.8 %multiply_reduce_fusion = (f32[512]{0:T(512)S(1)}, f32[512,1024]{1,0:T(8,128)}) fusion(bf16[512,4096]{1,0:T(8,128)(2,1)S(1)} %convolution_convert_fusion.1, bf16[4096,1024]{1,0:T(8,128)(2,1)S(1)} %bitcast.71), kind=kOutput, calls=%fused_computation.24 | convolution fusion | flops 4296015360 | bytes 14682112 | tf_op jit(solution)/shard_map/dot_general | solution.py:362
  80.3 8.9 %psum.14 = f32[2,512]{1,0:T(2,128)S(1)} all-reduce(f32[2,512]{1,0:T(2,128)S(1)} %pad_maximum_fusion), channel_id=1, replica_groups=mesh['tok'=8,'rep'=4] {'rep'}, use_global_device_ids=true, to_apply=%region_6.7 | all-reduce | flops 1024 | bytes 8192 | tf_op jit(solution)/shard_map/psum | solution.py:366
  89.3 1.6 multiply_multiply_fusion
  90.9 1.9 copy.29
  92.8 10.1 %convolution_convert_fusion.2 = bf16[512,1024]{1,0:T(8,128)(2,1)} fusion(bf16[512,4096]{1,0:T(8,128)(2,1)} %copy-done.13, bf16[4096,1024]{1,0:T(8,128)(2,1)} %param.16), kind=kOutput, calls=%fused_computation.26 | convolution fusion | flops 4295491584 | bytes 13631488 | tf_op jit(solution)/shard_map/dot_general | solution.py:367
  102.9 1.5 copy.32
  104.4 1.3 copy.33
  105.8 4.6 %all-to-all-start.2 = ((bf16[8,512,128]{2,1,0:T(8,128)(2,1)}), bf16[8,512,128]{2,1,0:T(8,128)(2,1)S(1)}, u32[]{:S(2)}, u32[]{:S(2)}) async-start(bf16[8,512,128]{2,1,0:T(8,128)(2,1)} %bitcast.54), calls=%async_computation.2 | async-start | bytes 2097152 | tf_op jit(solution)/shard_map/all_to_all | solution.py:376
  110.4 1.5 fusion.19
  111.9 1.8 copy.37
  113.7 3.2 copy.38
  116.9 3.1 multiply_multiply_fusion.1
  120.1 2.9 copy.25
  123.0 3.1 fusion.20
  126.1 3.2 copy.35
  129.2 3.1 copy.36
  132.4 2.8 multiply_subtract_fusion
  135.8 1.0 copy-done.2
  137.7 2.3 maximum_bitcast_fusion
  140.0 5.2 %all-to-all-start.1 = ((bf16[8,512,256]{2,1,0:T(8,128)(2,1)}), bf16[8,512,256]{2,1,0:T(8,128)(2,1)S(1)}, u32[]{:S(2)}, u32[]{:S(2)}) async-start(bf16[8,512,256]{2,1,0:T(8,128)(2,1)} %maximum_bitcast_fusion), calls=%async_computation.1 | async-start | bytes 4194304 | tf_op jit(solution)/shard_map/all_to_all | solution.py:383
  145.6 2.3 convert_reduce_fusion.1
  147.9 1.3 select_reduce_fusion.1
  149.3 2.3 copy.28
  151.5 42.7 %all-to-all-done.1.qk_ref = bf16[8,512,256]{2,1,0:T(8,128)(2,1)S(1)} async-done(((bf16[8,512,256]{2,1,0:T(8,128)(2,1)}), bf16[8,512,256]{2,1,0:T(8,128)(2,1)S(1)}, u32[]{:S(2)}, u32[]{:S(2)}) %all-to-all-start.1) | async-done | bytes 2097184 | tf_op jit(solution)/shard_map/all_to_all | solution.py:383
  194.3 19.8 %shard_map.139 = bf16[4096,128]{1,0:T(8,128)(2,1)S(1)} custom-call(s32[8]{0:T(128)S(1)} %bitcast_subtract_fusion.starts_ref, s32[8,1,512]{2,1,0:T(1,128)S(1)} %broadcast_in_dim.54.target_ref, bf16[8,512,256]{2,1,0:T(8,128)(2,1)S(1)} %all-to-all-done.1.qk_ref, bf16[8,512,128]{2,1,0:T(8,128)(2,1)S(1)} %all-to-all-done.2.v_ref), custom_call_target="tpu_custom_call" | custom-call | flops 6442450944 | bytes 4194304 | tf_op jit(solution)/shard_map/pallas_call | solution.py:263
  215.1 1.5 copy.34
  216.6 29.0 %all_to_all.30 = bf16[8,512,128]{1,2,0:T(8,128)(2,1)S(1)} all-to-all(bf16[8,512,128]{1,2,0:T(8,128)(2,1)S(1)} %copy.34), channel_id=1, replica_groups=mesh['tok'=8,'rep'=4] {'tok'}, dimensions={0} | all-to-all | bytes 2097152 | tf_op jit(solution)/shard_map/all_to_all | solution.py:408
  245.5 9.5 %fusion = bf16[4096,512]{0,1:T(8,128)(2,1)} fusion(bf16[512,1024]{0,1:T(8,128)(2,1)S(1)} %bitcast.63, bf16[1024,4096]{1,0:T(8,128)(2,1)} %param.17), kind=kOutput, calls=%fused_computation.8 | convolution fusion | flops 4297064448 | bytes 13631488 | tf_op jit(solution)/shard_map/dot_general | solution.py:418
  256.2 1.7 convolution_convert_fusion.4
  257.9 3.6 all-to-all-start.5
  261.5 1.7 convolution_convert_fusion.6
  263.3 24.7 %all-to-all-done.5 = bf16[8,64,1024]{2,1,0:T(8,128)(2,1)S(1)} async-done(((bf16[8,64,1024]{2,1,0:T(8,128)(2,1)}), bf16[8,64,1024]{2,1,0:T(8,128)(2,1)S(1)}, u32[]{:S(2)}, u32[]{:S(2)}) %all-to-all-start.5) | async-done | bytes 1048608 | tf_op jit(solution)/shard_map/all_to_all | solution.py:394
  288.0 3.6 all-to-all-start.4
  291.6 1.6 convert_reduce_fusion
  293.3 1.7 convolution_convert_fusion.8
  295.0 23.1 %all-to-all-done.4 = bf16[8,64,1024]{2,1,0:T(8,128)(2,1)S(1)} async-done(((bf16[8,64,1024]{2,1,0:T(8,128)(2,1)}), bf16[8,64,1024]{2,1,0:T(8,128)(2,1)S(1)}, u32[]{:S(2)}, u32[]{:S(2)}) %all-to-all-start.4) | async-done | bytes 1048608 | tf_op jit(solution)/shard_map/all_to_all | solution.py:394
  318.1 3.8 %all-to-all-start = ((bf16[8,64,1024]{2,1,0:T(8,128)(2,1)}), bf16[8,64,1024]{2,1,0:T(8,128)(2,1)S(1)}, u32[]{:S(2)}, u32[]{:S(2)}) async-start(bf16[8,64,1024]{2,1,0:T(8,128)(2,1)} %bitcast.58), calls=%async_computation | async-start | bytes 2097152 | tf_op jit(solution)/shard_map/all_to_all | solution.py:349
  322.0 2.4 select_reduce_fusion
  324.4 1.7 convolution_convert_fusion.3
  326.1 1.7 convolution_convert_fusion.5
  327.8 1.5 fusion.1
  329.3 8.9 %psum.15 = f32[512]{0:T(512)S(1)} all-reduce(f32[512]{0:T(512)S(1)} %fusion.1), channel_id=1, replica_groups=mesh['tok'=8,'rep'=4] {'rep'}, use_global_device_ids=true, to_apply=%region_11.12 | all-reduce | flops 512 | bytes 4096 | tf_op jit(solution)/shard_map/psum | solution.py:428
  338.1 10.0 %all-to-all-done = bf16[8,64,1024]{2,1,0:T(8,128)(2,1)S(1)} async-done(((bf16[8,64,1024]{2,1,0:T(8,128)(2,1)}), bf16[8,64,1024]{2,1,0:T(8,128)(2,1)S(1)}, u32[]{:S(2)}, u32[]{:S(2)}) %all-to-all-start) | async-done | bytes 1048608 | tf_op jit(solution)/shard_map/all_to_all | solution.py:349
  348.1 2.9 fusion.5
  (66 shorter events, 8.8 us)
Async XLA Ops:
  7.2 58.0 %all-gather.2.cloned.1.call-start = ((), (), s32[]{:S(2)}) async-start(), calls=%async_computation.7 | async-start | bytes 5242880 | tf_op jit(solution)/shard_map/all_gather | solution.py:314
  65.1 4.7 %copy-start.11 = (bf16[4096,1024]{1,0:T(8,128)(2,1)S(1)}, bf16[4096,1024]{1,0:T(8,128)(2,1)}, u32[]{:S(2)}) copy-start(bf16[4096,1024]{1,0:T(8,128)(2,1)} %param.14) | copy-start | bytes 25165828
  65.2 9.3 %slice-start = ((s8[8388608]{0:T(1024)(128)(4,1)}), s8[4194304]{0:T(1024)(128)(4,1)S(1)}, s32[]{:S(2)}) async-start(s8[8388608]{0:T(1024)(128)(4,1)} %bitcast.70), calls=%async_computation.9 | async-start | bytes 8388608
  69.8 4.6 %copy-start.13 = (bf16[512,4096]{1,0:T(8,128)(2,1)}, bf16[512,4096]{1,0:T(8,128)(2,1)S(1)}, u32[]{:S(2)}) copy-start(bf16[512,4096]{1,0:T(8,128)(2,1)S(1)} %convolution_convert_fusion.1) | copy-start | bytes 12582916
  69.9 4.6 %slice-start.1 = ((s8[8388608]{0:T(1024)(128)(4,1)}), s8[4194304]{0:T(1024)(128)(4,1)S(1)}, s32[]{:S(2)}) async-start(s8[8388608]{0:T(1024)(128)(4,1)} %bitcast.70), calls=%async_computation.10 | async-start | bytes 8388608
  74.5 14.8 %copy-start.9 = (f32[1024]{0:T(1024)S(1)}, f32[1024]{0:T(1024)}, u32[]{:S(2)}) copy-start(f32[1024]{0:T(1024)} %param.18) | copy-start | bytes 12292
  105.8 34.2 %all-to-all-start.2 = ((bf16[8,512,128]{2,1,0:T(8,128)(2,1)}), bf16[8,512,128]{2,1,0:T(8,128)(2,1)S(1)}, u32[]{:S(2)}, u32[]{:S(2)}) async-start(bf16[8,512,128]{2,1,0:T(8,128)(2,1)} %bitcast.54), calls=%async_computation.2 | async-start | bytes 2097152 | tf_op jit(solution)/shard_map/all_to_all | solution.py:376
  113.7 3.2 copy-start.10
  135.2 1.6 copy-start.2
  135.2 1.6 copy-start.3
  136.8 1.0 copy-start.1
  140.0 5.5 %copy-start.8 = (s32[4096]{0:T(1024)S(1)}, s32[4096]{0:T(1024)}, u32[]{:S(2)}) copy-start(s32[4096]{0:T(1024)} %param.23) | copy-start | bytes 49156
  140.0 54.3 %all-to-all-start.1 = ((bf16[8,512,256]{2,1,0:T(8,128)(2,1)}), bf16[8,512,256]{2,1,0:T(8,128)(2,1)S(1)}, u32[]{:S(2)}, u32[]{:S(2)}) async-start(bf16[8,512,256]{2,1,0:T(8,128)(2,1)} %maximum_bitcast_fusion), calls=%async_computation.1 | async-start | bytes 4194304 | tf_op jit(solution)/shard_map/all_to_all | solution.py:383
  145.2 182.5 %reduce-scatter.2.cloned.1.call-start = ((), (), s32[]{:S(2)}) async-start(), calls=%async_computation.8 | async-start | bytes 5242880 | tf_op jit(solution)/shard_map/reduce_scatter | solution.py:417
  214.1 1.0 copy-start
  255.0 1.2 copy-start.5
  256.2 5.3 %copy-start.6 = (bf16[512,8,128]{0,2,1:T(8,128)(2,1)S(1)}, bf16[512,8,128]{0,2,1:T(8,128)(2,1)}, u32[]{:S(2)}) copy-start(bf16[512,8,128]{0,2,1:T(8,128)(2,1)} %copy.28) | copy-start | bytes 3145732
  257.9 30.1 %all-to-all-start.5 = ((bf16[8,64,1024]{2,1,0:T(8,128)(2,1)}), bf16[8,64,1024]{2,1,0:T(8,128)(2,1)S(1)}, u32[]{:S(2)}, u32[]{:S(2)}) async-start(bf16[8,64,1024]{2,1,0:T(8,128)(2,1)} %bitcast.62), calls=%async_computation.6 | async-start | bytes 2097152 | tf_op jit(solution)/shard_map/all_to_all | solution.py:394
  261.5 30.1 %copy-start.7 = (s32[4096]{0:T(1024)S(1)}, s32[4096]{0:T(1024)}, u32[]{:S(2)}) copy-start(s32[4096]{0:T(1024)} %param.24) | copy-start | bytes 49156
  261.5 31.7 %copy-start.4 = (bf16[512,1024]{1,0:T(8,128)(2,1)S(1)}, bf16[512,1024]{1,0:T(8,128)(2,1)}, u32[]{:S(2)}) copy-start(bf16[512,1024]{1,0:T(8,128)(2,1)} %param.13) | copy-start | bytes 3145732
  288.0 30.1 %all-to-all-start.4 = ((bf16[8,64,1024]{2,1,0:T(8,128)(2,1)}), bf16[8,64,1024]{2,1,0:T(8,128)(2,1)S(1)}, u32[]{:S(2)}, u32[]{:S(2)}) async-start(bf16[8,64,1024]{2,1,0:T(8,128)(2,1)} %bitcast.61), calls=%async_computation.5 | async-start | bytes 2097152 | tf_op jit(solution)/shard_map/all_to_all | solution.py:394
  318.1 30.1 %all-to-all-start = ((bf16[8,64,1024]{2,1,0:T(8,128)(2,1)}), bf16[8,64,1024]{2,1,0:T(8,128)(2,1)S(1)}, u32[]{:S(2)}, u32[]{:S(2)}) async-start(bf16[8,64,1024]{2,1,0:T(8,128)(2,1)} %bitcast.58), calls=%async_computation | async-start | bytes 2097152 | tf_op jit(solution)/shard_map/all_to_all | solution.py:349
  326.1 22.0 %copy-start.12 = (f32[1024]{0:T(1024)S(1)}, f32[1024]{0:T(1024)}, u32[]{:S(2)}) copy-start(f32[1024]{0:T(1024)} %param.20) | copy-start | bytes 12292
Sparse Core Ops, SparseCore 0:
  9.8 55.2 all-gather.1
  255.2 50.5 reduce-scatter.1

commit v2 on v1

--- a/solution.py
+++ b/solution.py
@@ -197,22 +197,26 @@
     ).astype(jnp.bfloat16)
 
 
-def attend_kernel(starts_ref, target_ref, qk_ref, v_ref, out_ref, keys, values, *, size, head_size):
+def attend_kernel(
+    starts_ref, target_ref, qk_ref, v_ref, out_ref, keys, values, *, size, head_size, part, parts
+):
+    share = size // parts
+    skip = part * share
     block = pl.program_id(0)
     mine = pl.ds(pl.multiple_of(block * size, size), size)
     row_iota = lax.broadcasted_iota(jnp.int32, (size, size), 0)
-    column_iota = lax.broadcasted_iota(jnp.int32, (size, size), 1)
     hits = jnp.where(row_iota == target_ref[0], 1.0, 0.0).astype(jnp.bfloat16)
     qk_rows = qk_ref[...].reshape(size, 2 * head_size)
     v_rows = v_ref[...].reshape(size, head_size)
     packed_qk = jnp.dot(hits, qk_rows, preferred_element_type=jnp.float32).astype(jnp.bfloat16)
     packed_v = jnp.dot(hits, v_rows, preferred_element_type=jnp.float32).astype(jnp.bfloat16)
-    query = packed_qk[:, :head_size]
+    query = packed_qk[skip : skip + share, :head_size]
     keys[mine, :] = packed_qk[:, head_size:]
     values[mine, :] = packed_v
-    first = block * size
-    rows = first + lax.broadcasted_iota(jnp.int32, (size, 1), 0)
-    row_start = jnp.zeros((size, 1), jnp.int32)
+    base_row = block * size
+    first = base_row + skip
+    rows = first + lax.broadcasted_iota(jnp.int32, (share, 1), 0)
+    row_start = jnp.zeros((share, 1), jnp.int32)
     low = jnp.int32(0)
     for prompt in range(starts_ref.shape[0]):
         start = starts_ref[prompt]
@@ -225,8 +229,9 @@
             query, key_rows, (((1,), (1,)), ((), ())), preferred_element_type=jnp.float32
         ) * scale
 
-    local_start = row_start - first
-    allowed = (column_iota >= local_start) & (column_iota <= row_iota)
+    column_iota = lax.broadcasted_iota(jnp.int32, (share, size), 1)
+    row_iota = lax.broadcasted_iota(jnp.int32, (share, size), 0)
+    allowed = (column_iota >= row_start - base_row) & (column_iota <= row_iota + skip)
     scores = jnp.where(allowed, scores_of(packed_qk[:, head_size:]), -1e30)
     top = jnp.max(scores, axis=1, keepdims=True)
     weights = jnp.exp2(scores - top)
@@ -257,12 +262,14 @@
     out_ref[...] = (weighted / totals).astype(jnp.bfloat16)
 
 
-def attend_head(starts, target, qk_rows, v_rows):
+def attend_head(starts, target, qk_rows, v_rows, part, parts):
     shards, tok_rows, head_size = v_rows.shape
     chunk = tok_rows // shards
     return pl.pallas_call(
-        functools.partial(attend_kernel, size=tok_rows, head_size=head_size),
-        out_shape=jax.ShapeDtypeStruct((shards * tok_rows, head_size), jnp.bfloat16),
+        functools.partial(
+            attend_kernel, size=tok_rows, head_size=head_size, part=part, parts=parts
+        ),
+        out_shape=jax.ShapeDtypeStruct((shards * tok_rows // parts, head_size), jnp.bfloat16),
         grid_spec=pltpu.PrefetchScalarGridSpec(
             num_scalar_prefetch=1,
             grid=(shards,),
@@ -271,7 +278,7 @@
                 pl.BlockSpec((shards, chunk, 2 * head_size), lambda i, s: (0, i, 0)),
                 pl.BlockSpec((shards, chunk, head_size), lambda i, s: (0, i, 0)),
             ],
-            out_specs=pl.BlockSpec((tok_rows, head_size), lambda i, s: (i, 0)),
+            out_specs=pl.BlockSpec((tok_rows // parts, head_size), lambda i, s: (i, 0)),
             scratch_shapes=[
                 pltpu.VMEM((shards * tok_rows, head_size), jnp.bfloat16),
                 pltpu.VMEM((shards * tok_rows, head_size), jnp.bfloat16),
@@ -281,11 +288,87 @@
             dimension_semantics=("arbitrary",), vmem_limit_bytes=48 << 20
         ),
         cost_estimate=pl.CostEstimate(
-            flops=8 * tok_rows * tok_rows * shards * head_size * 3,
+            flops=8 * tok_rows * tok_rows * shards * head_size * 3 // parts,
             bytes_accessed=8 * shards * tok_rows * head_size,
             transcendentals=3 * shards * tok_rows * tok_rows,
         ),
     )(starts, target, qk_rows, v_rows)
+
+
+def rope_kernel(q_ref, k_ref, q_scale, k_scale, q_gain, k_gain, cosine, sine, qk_ref, key_ref):
+    head_size = q_ref.shape[1]
+
+    def turned(rows, scale, gain):
+        normed = rows[...] * scale[...] * gain[...]
+        other = pltpu.roll(normed, head_size // 2, 1)
+        return (normed * cosine[...] + other * sine[...]).astype(jnp.bfloat16)
+
+    qk_ref[0, :, :head_size] = turned(q_ref, q_scale, q_gain)
+    key_rows = turned(k_ref, k_scale, k_gain)
+    qk_ref[0, :, head_size:] = key_rows
+    key_ref[...] = key_rows
+
+
+def rope_heads(query_rows, key_rows, q_scale, k_scale, q_gain, k_gain, cosine, sine):
+    rows, width = query_rows.shape
+    head_size = cosine.shape[1]
+    heads = width // head_size
+    wide = pl.BlockSpec((rows, head_size), lambda h: (0, h))
+    thin = pl.BlockSpec((rows, 1), lambda h: (0, 0))
+    gain = pl.BlockSpec((1, head_size), lambda h: (0, h))
+    table = pl.BlockSpec((rows, head_size), lambda h: (0, 0))
+    return pl.pallas_call(
+        rope_kernel,
+        out_shape=(
+            jax.ShapeDtypeStruct((heads, rows, 2 * head_size), jnp.bfloat16),
+            jax.ShapeDtypeStruct((rows, width), jnp.bfloat16),
+        ),
+        grid=(heads,),
+        in_specs=[wide, wide, thin, thin, gain, gain, table, table],
+        out_specs=(pl.BlockSpec((1, rows, 2 * head_size), lambda h: (h, 0, 0)), wide),
+        compiler_params=pltpu.CompilerParams(vmem_limit_bytes=24 << 20),
+        cost_estimate=pl.CostEstimate(
+            flops=14 * rows * width, bytes_accessed=14 * rows * width, transcendentals=0
+        ),
+    )(query_rows, key_rows, q_scale, k_scale, q_gain, k_gain, cosine, sine)
+
+
+def value_kernel(x_ref, w_ref, flat_ref, heads_ref):
+    rows = jnp.dot(x_ref[...], w_ref[...], preferred_element_type=jnp.float32).astype(
+        jnp.bfloat16
+    )
+    flat_ref[...] = rows
+    count, _, head_size = heads_ref.shape
+    for head in range(count):
+        heads_ref[head] = rows[:, head * head_size : (head + 1) * head_size]
+
+
+def value_heads(pieces, w_value, head_size):
+    rows, depth = pieces.shape
+    width = w_value.shape[1]
+    count = 2
+    return pl.pallas_call(
+        value_kernel,
+        out_shape=(
+            jax.ShapeDtypeStruct((rows, width), jnp.bfloat16),
+            jax.ShapeDtypeStruct((width // head_size, rows, head_size), jnp.bfloat16),
+        ),
+        grid=(width // (count * head_size),),
+        in_specs=[
+            pl.BlockSpec((rows, depth), lambda h: (0, 0)),
+            pl.BlockSpec((depth, count * head_size), lambda h: (0, h)),
+        ],
+        out_specs=(
+            pl.BlockSpec((rows, count * head_size), lambda h: (0, h)),
+            pl.BlockSpec((count, rows, head_size), lambda h: (h, 0, 0)),
+        ),
+        compiler_params=pltpu.CompilerParams(vmem_limit_bytes=40 << 20),
+        cost_estimate=pl.CostEstimate(
+            flops=2 * rows * depth * width,
+            bytes_accessed=2 * (rows * depth + depth * width + 2 * rows * width),
+            transcendentals=0,
+        ),
+    )(pieces, w_value)
 
 
 def body_heads(
@@ -353,78 +436,83 @@
         concat_axis=0,
         tiled=True,
     )
+    half_size = head_size // 2
+    frequency = ROPE_BASE ** (-jnp.arange(half_size, dtype=jnp.float32) * 2.0 / head_size)
+    angles = positions.astype(jnp.float32)[:, None] * frequency[None, :]
+    cosine, sine = jnp.cos(angles), jnp.sin(angles)
+    cosine = jnp.concatenate([cosine, cosine], axis=1)
+    sine = jnp.concatenate([-sine, sine], axis=1)
+    pieces, sent_hidden, cosine, sine, target, slot_target = lax.optimization_barrier(
+        (pieces, sent_hidden, cosine, sine, target, slot_target)
+    )
     my_target = lax.dynamic_index_in_dim(target, me, 0, keepdims=False)
     my_hits = my_target[None, :] == local[:, None]
-    packed_hidden = select_rows(my_hits, sent_hidden.reshape(tok_rows, width_dev))
 
     pieces = select_rows(sort_hits, pieces)
+    value_half, value_sent = value_heads(pieces, w_value, head_size)
+
+    def exchange(rows):
+        return lax.all_to_all(rows, "tok", split_axis=0, concat_axis=0, tiled=True)
+
+    v_rows = exchange(value_sent)
+    pieces, value_half = lax.optimization_barrier((pieces, value_half))
     query_rows = jnp.dot(pieces, w_query, preferred_element_type=jnp.float32)
     key_rows = jnp.dot(pieces, w_key, preferred_element_type=jnp.float32)
     sums = jnp.stack(
         [jnp.sum(query_rows * query_rows, axis=1), jnp.sum(key_rows * key_rows, axis=1)]
     )
-    sums = lax.psum(sums, "rep")
-    value_half = jnp.dot(pieces, w_value, preferred_element_type=jnp.float32).astype(jnp.bfloat16)
-    query_rows = query_rows * lax.rsqrt(sums[0] / full_width + EPSILON)[:, None] * q_gain[None, :]
-    key_rows = key_rows * lax.rsqrt(sums[1] / full_width + EPSILON)[:, None] * k_gain[None, :]
-    query_rot = rotate(query_rows.reshape(tok_rows, heads_dev, head_size), positions).astype(
-        jnp.bfloat16
-    )
-    key_rot = rotate(key_rows.reshape(tok_rows, heads_dev, head_size), positions).astype(
-        jnp.bfloat16
-    )
-    v_rows = lax.all_to_all(
-        value_half.reshape(tok_rows, heads_dev, head_size).transpose(1, 0, 2),
-        "tok",
-        split_axis=0,
-        concat_axis=0,
-        tiled=True,
-    )
-    qk_rows = lax.all_to_all(
-        jnp.concatenate([query_rot, key_rot], axis=2).transpose(1, 0, 2),
-        "tok",
-        split_axis=0,
-        concat_axis=0,
-        tiled=True,
-    )
-    key_flat, value_half, qk_rows, v_rows = lax.optimization_barrier(
-        (key_rot.reshape(tok_rows, width_dev), value_half, qk_rows, v_rows)
-    )
-    sent_keys, sent_values = [
-        lax.all_to_all(
-            select_rows(slot_hits, rows).reshape(shards, chunk, width_dev),
-            "tok",
-            split_axis=0,
-            concat_axis=0,
-            tiled=True,
+    scales = lax.rsqrt(lax.psum(sums, "rep") / full_width + EPSILON)
+    qk_sent, key_flat = rope_heads(
+        query_rows,
+        key_rows,
+        scales[0][:, None],
+        scales[1][:, None],
+        q_gain[None, :],
+        k_gain[None, :],
+        cosine,
+        sine,
+    )
+    qk_rows = exchange(qk_sent)
+    qk_rows, v_rows, sent_hidden = lax.optimization_barrier((qk_rows, v_rows, sent_hidden))
+    packed_hidden = select_rows(my_hits, sent_hidden.reshape(tok_rows, width_dev))
+
+    parts = 2
+    share = tok_rows // parts
+    heads_out = [
+        attend_head(starts, target[:, None, :], qk_rows, v_rows, part, parts).reshape(
+            shards, share, head_size
+        )
+        for part in range(parts)
+    ]
+    first, last = lax.optimization_barrier((exchange(heads_out[0]), heads_out[1]))
+    attended = [first, exchange(last)]
+    attended[-1], key_flat, value_half = lax.optimization_barrier(
+        (attended[-1], key_flat, value_half)
+    )
+    mixed = []
+    for rows in attended:
+        rows = rows.transpose(1, 0, 2).reshape(share, width_dev)
+        mixed.append(
+            lax.psum_scatter(
+                lax.dot_general(
+                    w_out, rows, (((0,), (1,)), ((), ())), preferred_element_type=jnp.float32
+                ).astype(jnp.bfloat16),
+                "rep",
+                scatter_dimension=0,
+                tiled=True,
+            )
+        )
+    cache_hits = slot_target[None, :] == local[:, None]
+    cache_keys, cache_values = [
+        select_rows(
+            cache_hits,
+            exchange(select_rows(slot_hits, rows).reshape(shards, chunk, width_dev)).reshape(
+                tok_rows, width_dev
+            ),
         )
         for rows in (key_flat, value_half)
     ]
-    cache_hits = slot_target[None, :] == local[:, None]
-    cache_keys = select_rows(cache_hits, sent_keys.reshape(tok_rows, width_dev))
-    cache_values = select_rows(cache_hits, sent_values.reshape(tok_rows, width_dev))
-
-    attended = attend_head(starts, target[:, None, :], qk_rows, v_rows)
-    attended = lax.all_to_all(
-        attended.reshape(shards, tok_rows, head_size),
-        "tok",
-        split_axis=0,
-        concat_axis=0,
-        tiled=True,
-    )
-    attended = attended.transpose(1, 0, 2).reshape(tok_rows, width_dev)
-    mixed_rows = (
-        lax.psum_scatter(
-            lax.dot_general(
-                w_out, attended, (((0,), (1,)), ((), ())), preferred_element_type=jnp.float32
-            ).astype(jnp.bfloat16),
-            "rep",
-            scatter_dimension=0,
-            tiled=True,
-        )
-        .astype(jnp.float32)
-        .T
-    )
+    mixed_rows = jnp.concatenate([rows.astype(jnp.float32).T for rows in mixed], axis=0)
     mixed_sums = lax.psum(jnp.sum(mixed_rows * mixed_rows, axis=1), "rep")
     normed_rows = (
         mixed_rows * lax.rsqrt(mixed_sums / full_width + EPSILON)[:, None] * post_gain[None, :]

time: 359 us -> 326 us (0.908)
  blocking collectives: 46.8 us -> 17.8 us
  local copies, waits for them, and re-layouts: 32.3 us -> 8.14 us
  Pallas kernels: 19.8 us -> 41 us
  other arithmetic: 24.4 us -> 11.6 us
  starting transfers between devices: 21.1 us -> 30.6 us
    all_gather x1, waiting for transfers between devices: 51.8 us -> 20.4 us  [body_heads(): pieces = lax.all_gather(hidden_in, 'rep', axis=1, tiled=True)]
    all_to_all x1 -> x0, blocking collectives: 29 us -> none  [body_heads(): lax.all_to_all(attended.reshape(shards, tok_rows, head_size), 'tok', spli...]
    all_to_all x4 -> x6, waiting for transfers between devices: 90.6 us -> 116 us  [exchange(): return lax.all_to_all(rows, 'tok', split_axis=0, concat_axis=0, tiled=True)]
    pallas_call x0 -> x2, Pallas kernels: none -> 13.2 us  [the longest x1 9.44 us: value_heads(): pl.pallas_call(value_kernel, out_shape=(jax.ShapeDtypeStruct((rows, width...]
    unnamed x37 -> x33, local copies, waits for them, and re-layouts: 14.7 us -> 4.93 us
    pallas_call x1 -> x2, Pallas kernels: 19.8 us -> 27.8 us  [attend_head(): pl.pallas_call(functools.partial(attend_kernel, size=tok_rows, head_size=...]
    all_to_all x4 -> x6, starting transfers between devices: 17 us -> 23.9 us  [exchange(): return lax.all_to_all(rows, 'tok', split_axis=0, concat_axis=0, tiled=True)]
    all_to_all x1, waiting for transfers between devices: 9.98 us -> 16.7 us  [body_heads(): lax.all_to_all(select_rows(sort_hits, hidden_in).reshape(shards, chunk, w...]
  transfers between devices with their start and end apart: 7 -> 10, of which waited for: 5 -> 7; matrix products, arithmetic and copies ran while one was open for 15% -> 14% of each run, Pallas kernels for 0% -> 5%
where the time goes in v2:
time: 326 us; the launch traced here: 325 us
  waiting for transfers between devices  154 us (47%)
  matrix products  48.2 us (15%)
  Pallas kernels  41 us (13%)
  starting transfers between devices  30.6 us (9%)
  blocking collectives  17.8 us (5%)
  between operations  14.1 us (4%)
  other arithmetic  11.6 us (4%)
  local copies, waits for them, and re-layouts  8.14 us (2%)
    all_to_all x6, waiting for transfers between devices, exchange(): return lax.all_to_all(rows, 'tok', split_axis=0, concat_axis=0, tiled=True)  116 us
    pallas_call x2, Pallas kernels, attend_head(): pl.pallas_call(functools.partial(attend_kernel, size=tok_rows, head_size=...  27.8 us
    all_to_all x6, starting transfers between devices, exchange(): return lax.all_to_all(rows, 'tok', split_axis=0, concat_axis=0, tiled=True)  23.9 us
    all_gather x1, waiting for transfers between devices, body_heads(): pieces = lax.all_gather(hidden_in, 'rep', axis=1, tiled=True)  20.4 us
    dot_general x7, matrix products, select_rows(): jnp.dot(hits.astype(jnp.bfloat16), rows, preferred_element_type=jnp.float32)  17.1 us
    all_to_all x1, waiting for transfers between devices, body_heads(): lax.all_to_all(select_rows(sort_hits, hidden_in).reshape(shards, chunk, w...  16.7 us
    dot_general x2, matrix products, body_heads(): lax.dot_general(w_out, rows, (((0,), (1,)), ((), ())), preferred_element_...  14.3 us
    pallas_call x1, Pallas kernels, value_heads(): pl.pallas_call(value_kernel, out_shape=(jax.ShapeDtypeStruct((rows, width...  9.44 us
  transfers between devices with their start and end apart: 10, of which 7 were waited for; matrix products, arithmetic and copies ran while one was open for 14% of the time, Pallas kernels for 5%

profile of v2, /device:TPU:0, one launch (start us, length us, event | category | flops | bytes accessed | tf_op | source)
XLA Modules:
  0.0 325.4 jit_solution(15843498454551066502)
XLA Ops:
  7.2 0.7 all-gather.2.cloned.1.call-update
  7.9 0.8 dynamic_slice.10
  8.7 0.2 convert_reduce_fusion.3
  8.9 2.9 convolution_convert_fusion.8
  11.9 6.4 %all-to-all-start = ((bf16[8,64,1024]{2,1,0:T(8,128)(2,1)}), bf16[8,64,1024]{2,1,0:T(8,128)(2,1)S(1)}, u32[]{:S(2)}, u32[]{:S(2)}) async-start(bf16[8,64,1024]{2,1,0:T(8,128)(2,1)} %bitcast), calls=%async_computation | async-start | bytes 2097152 | tf_op jit(solution)/shard_map/all_to_all | solution.py:432
  18.5 1.6 convert_reduce_fusion
  20.3 0.4 select_reduce_fusion.2
  20.7 1.0 fusion.13
  22.1 2.3 convert_reduce_fusion.1
  24.3 1.3 select_reduce_fusion.1
  25.7 2.4 select_reduce_fusion
  28.1 16.7 %all-to-all-done = bf16[8,64,1024]{2,1,0:T(8,128)(2,1)S(1)} async-done(((bf16[8,64,1024]{2,1,0:T(8,128)(2,1)}), bf16[8,64,1024]{2,1,0:T(8,128)(2,1)S(1)}, u32[]{:S(2)}, u32[]{:S(2)}) %all-to-all-start) | async-done | bytes 1048608 | tf_op jit(solution)/shard_map/all_to_all | solution.py:432
  44.8 20.4 %all-gather.2.cloned.1.call-done = bf16[512,4096]{1,0:T(8,128)(2,1)} async-done(((bf16[512,1024]{1,0:T(8,128)(2,1)}), bf16[512,4096]{1,0:T(8,128)(2,1)}) %all-gather.2.cloned.1.call-update) | async-done | bytes 4194320 | tf_op jit(solution)/shard_map/all_gather | solution.py:397
  65.2 4.5 %convolution_convert_fusion.x_ref = bf16[512,4096]{1,0:T(8,128)(2,1)S(1)} fusion(bf16[512,4096]{1,0:T(8,128)(2,1)} %all-gather.2.cloned.1.call-done, s32[512]{0:T(512)S(1)} %convert_reduce_fusion.3), kind=kOutput, calls=%fused_computation.6 | convolution fusion | flops 2149842944 | bytes 8390656 | tf_op jit(solution)/shard_map/dot_general | solution.py:195
  69.8 9.4 %shard_map.139 = (bf16[512,1024]{1,0:T(8,128)(2,1)S(1)}, bf16[8,512,128]{2,1,0:T(8,128)(2,1)}) custom-call(bf16[512,4096]{1,0:T(8,128)(2,1)S(1)} %convolution_convert_fusion.x_ref, bf16[4096,1024]{1,0:T(8,128)(2,1)} %w_ref.1), custom_call_target="tpu_custom_call" | custom-call | flops 4294967296 | bytes 14680064 | tf_op jit(solution)/shard_map/pallas_call | solution.py:350
  79.2 1.0 copy-done.6
  80.2 4.6 %all-to-all-start.2 = ((bf16[8,512,128]{2,1,0:T(8,128)(2,1)}), bf16[8,512,128]{2,1,0:T(8,128)(2,1)}, u32[]{:S(2)}, u32[]{:S(2)}) async-start(bf16[8,512,128]{2,1,0:T(8,128)(2,1)} %get-tuple-element.30), calls=%async_computation.2 | async-start | bytes 2097152 | tf_op jit(solution)/shard_map/all_to_all | solution.py:455
  84.8 8.4 %multiply_reduce_fusion.1 = (f32[512]{0:T(512)S(1)}, f32[512,1024]{1,0:T(8,128)S(1)}) fusion(bf16[512,4096]{1,0:T(8,128)(2,1)} %copy-done.8, bf16[4096,1024]{1,0:T(8,128)(2,1)} %param.14), kind=kOutput, calls=%fused_computation.18 | convolution fusion | flops 4296015360 | bytes 14682112 | tf_op jit(solution)/shard_map/dot_general | solution.py:459
  93.3 8.4 %multiply_reduce_fusion = (f32[512]{0:T(512)S(1)}, f32[512,1024]{1,0:T(8,128)}) fusion(bf16[512,4096]{1,0:T(8,128)(2,1)S(1)} %copy-done.9, bf16[4096,1024]{1,0:T(8,128)(2,1)} %param.15), kind=kOutput, calls=%fused_computation.17 | convolution fusion | flops 4296015360 | bytes 14682112 | tf_op jit(solution)/shard_map/dot_general | solution.py:460
  101.7 8.9 %psum.14 = f32[2,512]{1,0:T(2,128)S(1)} all-reduce(f32[2,512]{1,0:T(2,128)S(1)} %pad_maximum_fusion.3), channel_id=1, replica_groups=mesh['tok'=8,'rep'=4] {'rep'}, use_global_device_ids=true, to_apply=%region_10.11 | all-reduce | flops 1024 | bytes 8192 | tf_op jit(solution)/shard_map/psum | solution.py:464
  111.0 1.6 copy-done
  112.6 3.8 %shard_map.140 = (bf16[8,512,256]{2,1,0:T(8,128)(2,1)S(1)}, bf16[512,1024]{1,0:T(8,128)(2,1)S(1)}) custom-call(f32[512,1024]{1,0:T(8,128)S(1)} %get-tuple-element.53.q_ref, f32[512,1024]{1,0:T(8,128)S(1)} %copy-done, f32[512,1]{1,0:T(8,128)S(1)} %copy.19.q_scale, f32[512,1]{1,0:T(8,128)S(1)} %copy.20.k_scale, f32[1,1024]{1,0:T(1,128)S(1)} %bitcast.52, ...), custom_call_target="tpu_custom_call" | custom-call | flops 7340032 | bytes 7340032 | tf_op jit(solution)/shard_map/pallas_call | solution.py:320
  116.4 1.3 copy-done.1
  117.8 1.0 copy-done.4
  118.7 5.1 %all-to-all-start.1 = ((bf16[8,512,256]{2,1,0:T(8,128)(2,1)}), bf16[8,512,256]{2,1,0:T(8,128)(2,1)S(1)}, u32[]{:S(2)}, u32[]{:S(2)}) async-start(bf16[8,512,256]{2,1,0:T(8,128)(2,1)} %copy-done.1), calls=%async_computation.1 | async-start | bytes 4194304 | tf_op jit(solution)/shard_map/all_to_all | solution.py:455
  123.8 49.0 %all-to-all-done.1.qk_ref = bf16[8,512,256]{2,1,0:T(8,128)(2,1)S(1)} async-done(((bf16[8,512,256]{2,1,0:T(8,128)(2,1)}), bf16[8,512,256]{2,1,0:T(8,128)(2,1)S(1)}, u32[]{:S(2)}, u32[]{:S(2)}) %all-to-all-start.1) | async-done | bytes 2097184 | tf_op jit(solution)/shard_map/all_to_all | solution.py:455
  172.9 15.2 %shard_map.141 = bf16[2048,128]{1,0:T(8,128)(2,1)S(1)} custom-call(s32[8]{0:T(128)S(1)} %bitcast_subtract_fusion.starts_ref, s32[8,1,512]{2,1,0:T(1,128)S(1)} %broadcast_in_dim.69.target_ref, bf16[8,512,256]{2,1,0:T(8,128)(2,1)S(1)} %all-to-all-done.1.qk_ref, bf16[8,512,128]{2,1,0:T(8,128)(2,1)} %all-to-all-done.2.v_ref), custom_call_target="tpu_custom_call" | custom-call | flops 3221225472 | bytes 4194304 | tf_op jit(solution)/shard_map/pallas_call | solution.py:268
  188.1 1.0 copy.21
  189.1 3.5 %all-to-all-start.3 = ((bf16[8,256,128]{1,2,0:T(8,128)(2,1)}), bf16[8,256,128]{1,2,0:T(8,128)(2,1)S(1)}, u32[]{:S(2)}, u32[]{:S(2)}) async-start(bf16[8,256,128]{1,2,0:T(8,128)(2,1)} %copy.21), calls=%async_computation.3 | async-start | bytes 1048576 | tf_op jit(solution)/shard_map/all_to_all | solution.py:455
  192.6 12.6 %shard_map.142 = bf16[2048,128]{1,0:T(8,128)(2,1)S(1)} custom-call(s32[8]{0:T(128)S(1)} %bitcast_subtract_fusion.starts_ref, s32[8,1,512]{2,1,0:T(1,128)S(1)} %broadcast_in_dim.69.target_ref, bf16[8,512,256]{2,1,0:T(8,128)(2,1)S(1)} %all-to-all-done.1.qk_ref, bf16[8,512,128]{2,1,0:T(8,128)(2,1)} %all-to-all-done.2.v_ref), custom_call_target="tpu_custom_call" | custom-call | flops 3221225472 | bytes 4194304 | tf_op jit(solution)/shard_map/pallas_call | solution.py:268
  205.2 2.6 all-to-all-done.3
  207.8 7.1 %fusion = bf16[4096,256]{0,1:T(8,128)(2,1)} fusion(bf16[256,1024]{0,1:T(8,128)(2,1)S(1)} %bitcast.54, bf16[1024,4096]{1,0:T(8,128)(2,1)} %param.17), kind=kOutput, calls=%fused_computation.9 | convolution fusion | flops 2148532224 | bytes 11010048 | tf_op jit(solution)/shard_map/dot_general | solution.py:497
  215.0 1.0 copy.22
  216.0 3.5 %all-to-all-start.4 = ((bf16[8,256,128]{1,2,0:T(8,128)(2,1)}), bf16[8,256,128]{1,2,0:T(8,128)(2,1)S(1)}, u32[]{:S(2)}, u32[]{:S(2)}) async-start(bf16[8,256,128]{1,2,0:T(8,128)(2,1)} %copy.22), calls=%async_computation.5 | async-start | bytes 1048576 | tf_op jit(solution)/shard_map/all_to_all | solution.py:455
  219.5 0.3 reduce-scatter.5.cloned.1.call-start
  220.0 14.7 %all-to-all-done.4 = bf16[8,256,128]{1,2,0:T(8,128)(2,1)S(1)} async-done(((bf16[8,256,128]{1,2,0:T(8,128)(2,1)}), bf16[8,256,128]{1,2,0:T(8,128)(2,1)S(1)}, u32[]{:S(2)}, u32[]{:S(2)}) %all-to-all-start.4) | async-done | bytes 524320 | tf_op jit(solution)/shard_map/all_to_all | solution.py:455
  234.7 7.1 %fusion.1 = bf16[4096,256]{0,1:T(8,128)(2,1)} fusion(bf16[256,1024]{0,1:T(8,128)(2,1)S(1)} %bitcast.55, bf16[1024,4096]{1,0:T(8,128)(2,1)} %param.17), kind=kOutput, calls=%fused_computation.10 | convolution fusion | flops 2148532224 | bytes 11010048 | tf_op jit(solution)/shard_map/dot_general | solution.py:497
  241.9 1.7 convolution_convert_fusion.4
  243.6 3.6 %all-to-all-start.6 = ((bf16[8,64,1024]{2,1,0:T(8,128)(2,1)}), bf16[8,64,1024]{2,1,0:T(8,128)(2,1)S(1)}, u32[]{:S(2)}, u32[]{:S(2)}) async-start(bf16[8,64,1024]{2,1,0:T(8,128)(2,1)} %bitcast.23), calls=%async_computation.8 | async-start | bytes 2097152 | tf_op jit(solution)/shard_map/all_to_all | solution.py:455
  247.2 1.7 convolution_convert_fusion.6
  248.9 24.8 %all-to-all-done.6 = bf16[8,64,1024]{2,1,0:T(8,128)(2,1)S(1)} async-done(((bf16[8,64,1024]{2,1,0:T(8,128)(2,1)}), bf16[8,64,1024]{2,1,0:T(8,128)(2,1)S(1)}, u32[]{:S(2)}, u32[]{:S(2)}) %all-to-all-start.6) | async-done | bytes 1048608 | tf_op jit(solution)/shard_map/all_to_all | solution.py:455
  273.7 3.7 %all-to-all-start.5 = ((bf16[8,64,1024]{2,1,0:T(8,128)(2,1)}), bf16[8,64,1024]{2,1,0:T(8,128)(2,1)S(1)}, u32[]{:S(2)}, u32[]{:S(2)}) async-start(bf16[8,64,1024]{2,1,0:T(8,128)(2,1)} %bitcast.21), calls=%async_computation.7 | async-start | bytes 2097152 | tf_op jit(solution)/shard_map/all_to_all | solution.py:455
  277.4 1.7 convolution_convert_fusion.3
  279.1 24.8 %all-to-all-done.5 = bf16[8,64,1024]{2,1,0:T(8,128)(2,1)S(1)} async-done(((bf16[8,64,1024]{2,1,0:T(8,128)(2,1)}), bf16[8,64,1024]{2,1,0:T(8,128)(2,1)S(1)}, u32[]{:S(2)}, u32[]{:S(2)}) %all-to-all-start.5) | async-done | bytes 1048608 | tf_op jit(solution)/shard_map/all_to_all | solution.py:455
  303.9 1.7 convolution_convert_fusion.5
  305.6 1.5 fusion.2
  307.0 8.9 %psum.15 = f32[512]{0:T(512)S(1)} all-reduce(f32[512]{0:T(512)S(1)} %fusion.2), channel_id=1, replica_groups=mesh['tok'=8,'rep'=4] {'rep'}, use_global_device_ids=true, to_apply=%region_14.15 | all-reduce | flops 512 | bytes 4096 | tf_op jit(solution)/shard_map/psum | solution.py:516
  315.9 2.9 fusion.5
  (62 shorter events, 1.6 us)
Async XLA Ops:
  7.2 11.1 %copy-start.12 = (s32[4096]{0:T(1024)S(1)}, s32[4096]{0:T(1024)}, u32[]{:S(2)}) copy-start(s32[4096]{0:T(1024)} %param.24) | copy-start | bytes 49156
  7.2 11.1 %copy-start.15 = (s32[8]{0:T(128)S(1)}, s32[8]{0:T(128)}, u32[]{:S(2)}) copy-start(s32[8]{0:T(128)} %param.21) | copy-start | bytes 100
  7.2 13.0 %copy-start.13 = (s32[4096]{0:T(1024)S(1)}, s32[4096]{0:T(1024)}, u32[]{:S(2)}) copy-start(s32[4096]{0:T(1024)} %param.23) | copy-start | bytes 49156
  7.2 58.0 %all-gather.2.cloned.1.call-start = ((), (), s32[]{:S(2)}) async-start(), calls=%async_computation.9 | async-start | bytes 5242880 | tf_op jit(solution)/shard_map/all_gather | solution.py:397
  11.9 32.9 %all-to-all-start = ((bf16[8,64,1024]{2,1,0:T(8,128)(2,1)}), bf16[8,64,1024]{2,1,0:T(8,128)(2,1)S(1)}, u32[]{:S(2)}, u32[]{:S(2)}) async-start(bf16[8,64,1024]{2,1,0:T(8,128)(2,1)} %bitcast), calls=%async_computation | async-start | bytes 2097152 | tf_op jit(solution)/shard_map/all_to_all | solution.py:432
  44.8 25.0 %copy-start.10 = (bf16[8,64,1024]{2,1,0:T(8,128)(2,1)}, bf16[8,64,1024]{2,1,0:T(8,128)(2,1)S(1)}, u32[]{:S(2)}) copy-start(bf16[8,64,1024]{2,1,0:T(8,128)(2,1)S(1)} %all-to-all-done) | copy-start | bytes 3145732
  69.7 9.4 %copy-start.8 = (bf16[512,4096]{1,0:T(8,128)(2,1)}, bf16[512,4096]{1,0:T(8,128)(2,1)S(1)}, u32[]{:S(2)}) copy-start(bf16[512,4096]{1,0:T(8,128)(2,1)S(1)} %convolution_convert_fusion.x_ref) | copy-start | bytes 12582916
  79.2 1.0 copy-start.6
  80.2 38.6 %all-to-all-start.2 = ((bf16[8,512,128]{2,1,0:T(8,128)(2,1)}), bf16[8,512,128]{2,1,0:T(8,128)(2,1)}, u32[]{:S(2)}, u32[]{:S(2)}) async-start(bf16[8,512,128]{2,1,0:T(8,128)(2,1)} %get-tuple-element.30), calls=%async_computation.2 | async-start | bytes 2097152 | tf_op jit(solution)/shard_map/all_to_all | solution.py:455
  84.8 8.5 %copy-start.9 = (bf16[512,4096]{1,0:T(8,128)(2,1)S(1)}, bf16[512,4096]{1,0:T(8,128)(2,1)}, u32[]{:S(2)}) copy-start(bf16[512,4096]{1,0:T(8,128)(2,1)} %copy-done.8) | copy-start | bytes 12582916
  93.3 17.7 %copy-start.2 = (f32[1024]{0:T(1024)S(1)}, f32[1024]{0:T(1024)}, u32[]{:S(2)}) copy-start(f32[1024]{0:T(1024)} %param.18) | copy-start | bytes 12292
  93.3 17.7 %copy-start.3 = (f32[1024]{0:T(1024)S(1)}, f32[1024]{0:T(1024)}, u32[]{:S(2)}) copy-start(f32[1024]{0:T(1024)} %param.19) | copy-start | bytes 12292
  111.0 1.6 copy-start
  116.4 1.4 copy-start.1
  117.8 1.0 copy-start.4
  118.7 54.1 %all-to-all-start.1 = ((bf16[8,512,256]{2,1,0:T(8,128)(2,1)}), bf16[8,512,256]{2,1,0:T(8,128)(2,1)S(1)}, u32[]{:S(2)}, u32[]{:S(2)}) async-start(bf16[8,512,256]{2,1,0:T(8,128)(2,1)} %copy-done.1), calls=%async_computation.1 | async-start | bytes 4194304 | tf_op jit(solution)/shard_map/all_to_all | solution.py:455
  189.1 18.8 %all-to-all-start.3 = ((bf16[8,256,128]{1,2,0:T(8,128)(2,1)}), bf16[8,256,128]{1,2,0:T(8,128)(2,1)S(1)}, u32[]{:S(2)}, u32[]{:S(2)}) async-start(bf16[8,256,128]{1,2,0:T(8,128)(2,1)} %copy.21), calls=%async_computation.3 | async-start | bytes 1048576 | tf_op jit(solution)/shard_map/all_to_all | solution.py:455
  192.6 113.0 %reduce-scatter.3.cloned.1.call-start = ((), (), s32[]{:S(2)}) async-start(), calls=%async_computation.10 | async-start | bytes 2621440 | tf_op jit(solution)/shard_map/reduce_scatter | solution.py:496
  216.0 18.8 %all-to-all-start.4 = ((bf16[8,256,128]{1,2,0:T(8,128)(2,1)}), bf16[8,256,128]{1,2,0:T(8,128)(2,1)S(1)}, u32[]{:S(2)}, u32[]{:S(2)}) async-start(bf16[8,256,128]{1,2,0:T(8,128)(2,1)} %copy.22), calls=%async_computation.5 | async-start | bytes 1048576 | tf_op jit(solution)/shard_map/all_to_all | solution.py:455
  219.5 86.1 %reduce-scatter.5.cloned.1.call-start = ((), (), s32[]{:S(2)}) async-start(), calls=%async_computation.11 | async-start | bytes 2621440 | tf_op jit(solution)/shard_map/reduce_scatter | solution.py:496
  234.7 7.2 %copy-start.7 = (bf16[512,1024]{1,0:T(8,128)(2,1)S(1)}, bf16[512,1024]{1,0:T(8,128)(2,1)}, u32[]{:S(2)}) copy-start(bf16[512,1024]{1,0:T(8,128)(2,1)} %copy-done.6) | copy-start | bytes 3145732
  241.9 5.3 %copy-start.5 = (bf16[512,1024]{1,0:T(8,128)(2,1)S(1)}, bf16[512,1024]{1,0:T(8,128)(2,1)}, u32[]{:S(2)}) copy-start(bf16[512,1024]{1,0:T(8,128)(2,1)} %copy-done.4) | copy-start | bytes 3145732
  243.6 30.1 %all-to-all-start.6 = ((bf16[8,64,1024]{2,1,0:T(8,128)(2,1)}), bf16[8,64,1024]{2,1,0:T(8,128)(2,1)S(1)}, u32[]{:S(2)}, u32[]{:S(2)}) async-start(bf16[8,64,1024]{2,1,0:T(8,128)(2,1)} %bitcast.23), calls=%async_computation.8 | async-start | bytes 2097152 | tf_op jit(solution)/shard_map/all_to_all | solution.py:455
  273.7 42.2 %copy-start.11 = (bf16[8,64,1024]{2,1,0:T(8,128)(2,1)S(1)}, bf16[8,64,1024]{2,1,0:T(8,128)(2,1)}, u32[]{:S(2)}) copy-start(bf16[8,64,1024]{2,1,0:T(8,128)(2,1)} %copy-done.10) | copy-start | bytes 3145732
  273.7 42.2 %copy-start.14 = (f32[1024]{0:T(1024)S(1)}, f32[1024]{0:T(1024)}, u32[]{:S(2)}) copy-start(f32[1024]{0:T(1024)} %param.20) | copy-start | bytes 12292
  273.7 30.2 %all-to-all-start.5 = ((bf16[8,64,1024]{2,1,0:T(8,128)(2,1)}), bf16[8,64,1024]{2,1,0:T(8,128)(2,1)S(1)}, u32[]{:S(2)}, u32[]{:S(2)}) async-start(bf16[8,64,1024]{2,1,0:T(8,128)(2,1)} %bitcast.21), calls=%async_computation.7 | async-start | bytes 2097152 | tf_op jit(solution)/shard_map/all_to_all | solution.py:455
Sparse Core Ops, SparseCore 0:
  9.8 55.3 all-gather.1
  215.1 33.0 reduce-scatter.2
  251.2 35.1 reduce-scatter.4

commit v3 on v2

--- a/solution.py
+++ b/solution.py
@@ -333,17 +333,16 @@
     )(query_rows, key_rows, q_scale, k_scale, q_gain, k_gain, cosine, sine)
 
 
-def value_kernel(x_ref, w_ref, flat_ref, heads_ref):
-    rows = jnp.dot(x_ref[...], w_ref[...], preferred_element_type=jnp.float32).astype(
-        jnp.bfloat16
-    )
+def value_kernel(owner_ref, x_ref, w_ref, so_far_ref, flat_ref, heads_ref):
+    rows = so_far_ref[...] + jnp.dot(x_ref[...], w_ref[...], preferred_element_type=jnp.float32)
+    rows = rows.astype(jnp.bfloat16)
     flat_ref[...] = rows
     count, _, head_size = heads_ref.shape
     for head in range(count):
         heads_ref[head] = rows[:, head * head_size : (head + 1) * head_size]
 
 
-def value_heads(pieces, w_value, head_size):
+def value_heads(owner, pieces, w_value, so_far, head_size):
     rows, depth = pieces.shape
     width = w_value.shape[1]
     count = 2
@@ -353,14 +352,18 @@
             jax.ShapeDtypeStruct((rows, width), jnp.bfloat16),
             jax.ShapeDtypeStruct((width // head_size, rows, head_size), jnp.bfloat16),
         ),
-        grid=(width // (count * head_size),),
-        in_specs=[
-            pl.BlockSpec((rows, depth), lambda h: (0, 0)),
-            pl.BlockSpec((depth, count * head_size), lambda h: (0, h)),
-        ],
-        out_specs=(
-            pl.BlockSpec((rows, count * head_size), lambda h: (0, h)),
-            pl.BlockSpec((count, rows, head_size), lambda h: (h, 0, 0)),
+        grid_spec=pltpu.PrefetchScalarGridSpec(
+            num_scalar_prefetch=1,
+            grid=(width // (count * head_size),),
+            in_specs=[
+                pl.BlockSpec((rows, depth), lambda h, owner: (0, 0)),
+                pl.BlockSpec((depth, count * head_size), lambda h, owner: (owner[0], h)),
+                pl.BlockSpec((rows, count * head_size), lambda h, owner: (0, h)),
+            ],
+            out_specs=(
+                pl.BlockSpec((rows, count * head_size), lambda h, owner: (0, h)),
+                pl.BlockSpec((count, rows, head_size), lambda h, owner: (h, 0, 0)),
+            ),
         ),
         compiler_params=pltpu.CompilerParams(vmem_limit_bytes=40 << 20),
         cost_estimate=pl.CostEstimate(
@@ -368,7 +371,7 @@
             bytes_accessed=2 * (rows * depth + depth * width + 2 * rows * width),
             transcendentals=0,
         ),
-    )(pieces, w_value)
+    )(owner, pieces, w_value, so_far)
 
 
 def body_heads(
@@ -394,7 +397,10 @@
     chunk = tok_rows // shards
     me = lax.axis_index("tok")
     first_row = me * tok_rows
-    pieces = lax.all_gather(hidden_in, "rep", axis=1, tiled=True)
+    half_rows = tok_rows // 2
+    corner = lax.axis_index("rep")
+    across = [(i, i ^ 1) for i in range(4)]
+    along = [(i, i ^ 2) for i in range(4)]
 
     local = jnp.arange(tok_rows, dtype=jnp.int32)
     starts = jnp.cumsum(prompt_lengths) - prompt_lengths
@@ -429,8 +435,30 @@
         jnp.where(landed[:, None] == local[None, :], slot_rows.reshape(-1)[:, None], 0), axis=0
     )
 
+    piece = select_rows(sort_hits, hidden_in)
+    piece_x = lax.ppermute(piece, "rep", across)
+    piece_y = lax.ppermute(piece, "rep", along)
+    piece_xy = jnp.concatenate(
+        [
+            lax.ppermute(piece_y[:half_rows], "rep", across),
+            lax.ppermute(piece_x[half_rows:], "rep", along),
+        ],
+        axis=0,
+    )
+
+    def product(rows, weights, step):
+        owned = lax.dynamic_slice_in_dim(weights, (corner ^ step) * width_dev, width_dev, axis=0)
+        return jnp.dot(rows, owned, preferred_element_type=jnp.float32)
+
+    sums_now = [product(piece, weights, 0) for weights in (w_value, w_query, w_key)]
+    for step, rows in ((1, piece_x), (2, piece_y)):
+        sums_now = [
+            done + product(rows, weights, step)
+            for done, weights in zip(sums_now, (w_value, w_query, w_key))
+        ]
+
     sent_hidden = lax.all_to_all(
-        select_rows(sort_hits, hidden_in).reshape(shards, chunk, width_dev),
+        piece.reshape(shards, chunk, width_dev),
         "tok",
         split_axis=0,
         concat_axis=0,
@@ -442,22 +470,22 @@
     cosine, sine = jnp.cos(angles), jnp.sin(angles)
     cosine = jnp.concatenate([cosine, cosine], axis=1)
     sine = jnp.concatenate([-sine, sine], axis=1)
-    pieces, sent_hidden, cosine, sine, target, slot_target = lax.optimization_barrier(
-        (pieces, sent_hidden, cosine, sine, target, slot_target)
+    piece_xy, sent_hidden, cosine, sine, target, slot_target, sums_now = lax.optimization_barrier(
+        (piece_xy, sent_hidden, cosine, sine, target, slot_target, sums_now)
     )
     my_target = lax.dynamic_index_in_dim(target, me, 0, keepdims=False)
     my_hits = my_target[None, :] == local[:, None]
 
-    pieces = select_rows(sort_hits, pieces)
-    value_half, value_sent = value_heads(pieces, w_value, head_size)
+    last = corner ^ 3
+    value_half, value_sent = value_heads(last[None], piece_xy, w_value, sums_now[0], head_size)
 
     def exchange(rows):
         return lax.all_to_all(rows, "tok", split_axis=0, concat_axis=0, tiled=True)
 
     v_rows = exchange(value_sent)
-    pieces, value_half = lax.optimization_barrier((pieces, value_half))
-    query_rows = jnp.dot(pieces, w_query, preferred_element_type=jnp.float32)
-    key_rows = jnp.dot(pieces, w_key, preferred_element_type=jnp.float32)
+    piece_xy, value_half = lax.optimization_barrier((piece_xy, value_half))
+    query_rows = sums_now[1] + product(piece_xy, w_query, 3)
+    key_rows = sums_now[2] + product(piece_xy, w_key, 3)
     sums = jnp.stack(
         [jnp.sum(query_rows * query_rows, axis=1), jnp.sum(key_rows * key_rows, axis=1)]
     )
@@ -524,7 +552,8 @@
 def solution(mesh):
     def pick(*operands):
         heads_dev = operands[0].shape[1] // HEAD_DIM
-        chosen = body_heads if heads_dev == mesh.shape["tok"] else body
+        fits = heads_dev == mesh.shape["tok"] and mesh.shape["rep"] == 4
+        chosen = body_heads if fits else body
         return chosen(*operands)
 
     return jax.shard_map(

time: 326 us -> 318 us (0.975)
  waiting for transfers between devices: 154 us -> 115 us
  local copies, waits for them, and re-layouts: 8.14 us -> 24.5 us
  matrix products: 48.2 us -> 59.6 us
  Pallas kernels: 41 us -> 34.6 us
  starting transfers between devices: 30.6 us -> 35.6 us
  other arithmetic: 11.6 us -> 16.5 us
    all_gather x1 -> x0, waiting for transfers between devices: 20.4 us -> none  [body_heads(): pieces = lax.all_gather(hidden_in, 'rep', axis=1, tiled=True)]
    all_to_all x1, waiting for transfers between devices: 16.7 us -> 0.01 us  [body_heads(): lax.all_to_all(piece.reshape(shards, chunk, width_dev), 'tok', split_axis...]
    dot_general x2 -> x11, matrix products: 16.9 us -> 33.5 us  [product(): return jnp.dot(rows, owned, preferred_element_type=jnp.float32)]
    unnamed x33 -> x59, local copies, waits for them, and re-layouts: 4.93 us -> 17.3 us
    pallas_call x1, Pallas kernels: 9.44 us -> 2.38 us  [value_heads(): pl.pallas_call(value_kernel, out_shape=(jax.ShapeDtypeStruct((rows, width...]
    ppermute x0 -> x4, starting transfers between devices: none -> 5.67 us  [the longest x1 2.97 us: body_heads(): piece_x = lax.ppermute(piece, 'rep', across)]
    dot_general x7 -> x6, matrix products: 17.1 us -> 11.8 us  [select_rows(): jnp.dot(hits.astype(jnp.bfloat16), rows, preferred_element_type=jnp.float32)]
  transfers between devices with their start and end apart: 10 -> 13, of which waited for: 7 -> 5; matrix products, arithmetic and copies ran while one was open for 14% -> 21% of each run, Pallas kernels for 5% -> 5%
where the time goes in v3:
time: 318 us
  waiting for transfers between devices  115 us (36%)
  matrix products  59.6 us (19%)
  starting transfers between devices  35.6 us (11%)
  Pallas kernels  34.6 us (11%)
  local copies, waits for them, and re-layouts  24.5 us (8%)
  blocking collectives  17.8 us (6%)
  other arithmetic  16.5 us (5%)
  between operations  14.5 us (5%)
    all_to_all x6, waiting for transfers between devices, exchange(): return lax.all_to_all(rows, 'tok', split_axis=0, concat_axis=0, tiled=True)  115 us
    dot_general x11, matrix products, product(): return jnp.dot(rows, owned, preferred_element_type=jnp.float32)  33.5 us
    pallas_call x2, Pallas kernels, attend_head(): pl.pallas_call(functools.partial(attend_kernel, size=tok_rows, head_size=...  28.5 us
    all_to_all x6, starting transfers between devices, exchange(): return lax.all_to_all(rows, 'tok', split_axis=0, concat_axis=0, tiled=True)  25 us
    unnamed x59, local copies, waits for them, and re-layouts  17.3 us
    dot_general x2, matrix products, body_heads(): lax.dot_general(w_out, rows, (((0,), (1,)), ((), ())), preferred_element_...  14.4 us
    dot_general x6, matrix products, select_rows(): jnp.dot(hits.astype(jnp.bfloat16), rows, preferred_element_type=jnp.float32)  11.8 us
    psum x1, blocking collectives, body_heads(): scales = lax.rsqrt(lax.psum(sums, 'rep') / full_width + EPSILON)  9.59 us
  transfers between devices with their start and end apart: 13, of which 5 were waited for; matrix products, arithmetic and copies ran while one was open for 21% of the time, Pallas kernels for 5%

profile of v3, /device:TPU:0, one launch (start us, length us, event | category | flops | bytes accessed | tf_op | source)
XLA Modules:
  0.0 318.3 jit_solution(8406696995278238087)
XLA Ops:
  8.4 1.7 convolution_convert_fusion.7
  10.1 3.0 collective-permute-start.2
  13.1 1.5 collective-permute-start
  14.6 4.9 %all-to-all-start = ((bf16[8,64,1024]{2,1,0:T(8,128)(2,1)}), bf16[8,64,1024]{2,1,0:T(8,128)(2,1)}, u32[]{:S(2)}, u32[]{:S(2)}) async-start(bf16[8,64,1024]{2,1,0:T(8,128)(2,1)} %bitcast), calls=%async_computation | async-start | bytes 2097152 | tf_op jit(solution)/shard_map/all_to_all | solution.py:460
  20.3 4.5 %fusion.14 = f32[512,1024]{1,0:T(8,128)} fusion(bf16[512,1024]{1,0:T(8,128)(2,1)} %convolution_convert_fusion.7, bf16[4096,1024]{1,0:T(8,128)(2,1)} %param.15, s32[]{:T(128)S(6)} %select_n.75), kind=kOutput, calls=%fused_computation.27 | convolution fusion | flops 1073741824 | bytes 5242884 | tf_op jit(solution)/shard_map/dot_general | solution.py:451
  24.9 3.2 fusion.20
  28.1 1.6 convert_reduce_fusion
  29.8 2.3 convert_reduce_fusion.1
  32.1 1.9 fusion.40
  34.0 2.1 pad_maximum_fusion.2
  36.1 3.3 %fusion.26 = f32[512,1024]{1,0:T(8,128)S(1)} fusion(bf16[512,1024]{1,0:T(8,128)(2,1)} %convolution_convert_fusion.7, bf16[4096,1024]{1,0:T(8,128)(2,1)} %w_ref.1, s32[]{:T(128)S(6)} %select_n.75), kind=kOutput, calls=%fused_computation.41 | convolution fusion | flops 1073741824 | bytes 5242884 | tf_op jit(solution)/shard_map/dot_general | solution.py:451
  40.7 2.6 select_reduce_fusion
  45.9 3.2 fusion.12
  49.1 2.6 fusion.18
  51.8 4.4 %add_add_fusion = f32[512,1024]{1,0:T(8,128)} fusion(f32[512,1024]{1,0:T(8,128)S(1)} %copy-done.20, f32[512,1024]{1,0:T(8,128)S(1)} %fusion.12, bf16[512,1024]{1,0:T(8,128)(2,1)S(1)} %collective-permute-done, bf16[4096,1024]{1,0:T(8,128)(2,1)} %param.15, s32[]{:T(128)S(6)} %select_n.77), kind=kOutput, calls=%fused_computation.24 | convolution fusion | flops 1074790400 | bytes 9437188 | tf_op jit(solution)/shard_map/dot_general | solution.py:451
  56.2 2.7 add_add_fusion.1
  58.8 2.5 fusion.24
  62.8 3.4 %copy-done.2 = bf16[4096,1024]{1,0:T(8,128)(2,1)S(1)} copy-done((bf16[4096,1024]{1,0:T(8,128)(2,1)S(1)}, bf16[4096,1024]{1,0:T(8,128)(2,1)}, u32[]{:S(2)}) %copy-start.2) | copy-done | bytes 8388632
  66.1 2.4 shard_map.139
  70.5 5.1 %all-to-all-start.2 = ((bf16[8,512,128]{2,1,0:T(8,128)(2,1)}), bf16[8,512,128]{2,1,0:T(8,128)(2,1)}, u32[]{:S(2)}, u32[]{:S(2)}) async-start(bf16[8,512,128]{2,1,0:T(8,128)(2,1)} %copy-done.8), calls=%async_computation.2 | async-start | bytes 2097152 | tf_op jit(solution)/shard_map/all_to_all | solution.py:483
  75.6 2.8 fusion.6
  78.4 3.0 fusion.8
  83.0 1.6 multiply_reduce_fusion.1
  84.6 9.6 %psum.14 = f32[2,512]{1,0:T(2,128)S(1)} all-reduce(f32[2,512]{1,0:T(2,128)S(1)} %pad_maximum_fusion.4), channel_id=1, replica_groups=mesh['tok'=8,'rep'=4] {'rep'}, use_global_device_ids=true, to_apply=%region_10.11 | all-reduce | flops 1024 | bytes 8192 | tf_op jit(solution)/shard_map/psum | solution.py:492
  95.9 1.6 copy-done.3
  100.4 3.7 %shard_map.140 = (bf16[8,512,256]{2,1,0:T(8,128)(2,1)S(1)}, bf16[512,1024]{1,0:T(8,128)(2,1)S(1)}) custom-call(f32[512,1024]{1,0:T(8,128)S(1)} %copy-done.3, f32[512,1024]{1,0:T(8,128)S(1)} %get-tuple-element.54.k_ref, f32[512,1]{1,0:T(8,128)S(1)} %copy-done.6, f32[512,1]{1,0:T(8,128)S(1)} %copy-done.7, f32[1,1024]{1,0:T(1,128)S(1)} %bitcast.61, ...), custom_call_target="tpu_custom_call" | custom-call | flops 7340032 | bytes 7340032 | tf_op jit(solution)/shard_map/pallas_call | solution.py:320
  106.4 5.1 %all-to-all-start.1 = ((bf16[8,512,256]{2,1,0:T(8,128)(2,1)}), bf16[8,512,256]{2,1,0:T(8,128)(2,1)S(1)}, u32[]{:S(2)}, u32[]{:S(2)}) async-start(bf16[8,512,256]{2,1,0:T(8,128)(2,1)} %copy-done.4), calls=%async_computation.1 | async-start | bytes 4194304 | tf_op jit(solution)/shard_map/all_to_all | solution.py:483
  111.5 49.0 %all-to-all-done.1.qk_ref = bf16[8,512,256]{2,1,0:T(8,128)(2,1)S(1)} async-done(((bf16[8,512,256]{2,1,0:T(8,128)(2,1)}), bf16[8,512,256]{2,1,0:T(8,128)(2,1)S(1)}, u32[]{:S(2)}, u32[]{:S(2)}) %all-to-all-start.1) | async-done | bytes 2097184 | tf_op jit(solution)/shard_map/all_to_all | solution.py:483
  160.5 15.7 %shard_map.141 = bf16[2048,128]{1,0:T(8,128)(2,1)S(1)} custom-call(s32[8]{0:T(128)S(1)} %bitcast_subtract_fusion.starts_ref, s32[8,1,512]{2,1,0:T(1,128)S(1)} %broadcast_in_dim.110.target_ref, bf16[8,512,256]{2,1,0:T(8,128)(2,1)S(1)} %all-to-all-done.1.qk_ref, bf16[8,512,128]{2,1,0:T(8,128)(2,1)} %all-to-all-done.2.v_ref), custom_call_target="tpu_custom_call" | custom-call | flops 3221225472 | bytes 4194304 | tf_op jit(solution)/shard_map/pallas_call | solution.py:268
  177.0 2.0 copy.21
  179.0 4.2 %all-to-all-start.3 = ((bf16[8,256,128]{1,2,0:T(8,128)(2,1)}), bf16[8,256,128]{1,2,0:T(8,128)(2,1)}, u32[]{:S(2)}, u32[]{:S(2)}) async-start(bf16[8,256,128]{1,2,0:T(8,128)(2,1)} %copy.21), calls=%async_computation.3 | async-start | bytes 1048576 | tf_op jit(solution)/shard_map/all_to_all | solution.py:483
  183.2 12.8 %shard_map.142 = bf16[2048,128]{1,0:T(8,128)(2,1)S(1)} custom-call(s32[8]{0:T(128)S(1)} %bitcast_subtract_fusion.starts_ref, s32[8,1,512]{2,1,0:T(1,128)S(1)} %broadcast_in_dim.110.target_ref, bf16[8,512,256]{2,1,0:T(8,128)(2,1)S(1)} %all-to-all-done.1.qk_ref, bf16[8,512,128]{2,1,0:T(8,128)(2,1)} %all-to-all-done.2.v_ref), custom_call_target="tpu_custom_call" | custom-call | flops 3221225472 | bytes 4194304 | tf_op jit(solution)/shard_map/pallas_call | solution.py:268
  196.9 1.6 all-to-all-done.3
  198.5 7.3 %fusion = bf16[4096,256]{0,1:T(8,128)(2,1)} fusion(bf16[256,1024]{0,1:T(8,128)(2,1)} %bitcast.15, bf16[1024,4096]{1,0:T(8,128)(2,1)} %param.17), kind=kOutput, calls=%fused_computation.8 | convolution fusion | flops 2148532224 | bytes 11010048 | tf_op jit(solution)/shard_map/dot_general | solution.py:525
  207.9 3.5 %all-to-all-start.4 = ((bf16[8,256,128]{1,2,0:T(8,128)(2,1)}), bf16[8,256,128]{1,2,0:T(8,128)(2,1)S(1)}, u32[]{:S(2)}, u32[]{:S(2)}) async-start(bf16[8,256,128]{1,2,0:T(8,128)(2,1)} %copy.22), calls=%async_computation.5 | async-start | bytes 1048576 | tf_op jit(solution)/shard_map/all_to_all | solution.py:483
  211.7 15.0 %all-to-all-done.4 = bf16[8,256,128]{1,2,0:T(8,128)(2,1)S(1)} async-done(((bf16[8,256,128]{1,2,0:T(8,128)(2,1)}), bf16[8,256,128]{1,2,0:T(8,128)(2,1)S(1)}, u32[]{:S(2)}, u32[]{:S(2)}) %all-to-all-start.4) | async-done | bytes 524320 | tf_op jit(solution)/shard_map/all_to_all | solution.py:483
  226.6 7.1 %fusion.1 = bf16[4096,256]{0,1:T(8,128)(2,1)} fusion(bf16[256,1024]{0,1:T(8,128)(2,1)S(1)} %bitcast.63, bf16[1024,4096]{1,0:T(8,128)(2,1)} %param.17), kind=kOutput, calls=%fused_computation.9 | convolution fusion | flops 2148532224 | bytes 11010048 | tf_op jit(solution)/shard_map/dot_general | solution.py:525
  234.9 1.7 convolution_convert_fusion.3
  236.6 3.6 %all-to-all-start.6 = ((bf16[8,64,1024]{2,1,0:T(8,128)(2,1)}), bf16[8,64,1024]{2,1,0:T(8,128)(2,1)S(1)}, u32[]{:S(2)}, u32[]{:S(2)}) async-start(bf16[8,64,1024]{2,1,0:T(8,128)(2,1)} %bitcast.24), calls=%async_computation.8 | async-start | bytes 2097152 | tf_op jit(solution)/shard_map/all_to_all | solution.py:483
  240.2 1.7 convolution_convert_fusion.5
  241.9 24.8 %all-to-all-done.6 = bf16[8,64,1024]{2,1,0:T(8,128)(2,1)S(1)} async-done(((bf16[8,64,1024]{2,1,0:T(8,128)(2,1)}), bf16[8,64,1024]{2,1,0:T(8,128)(2,1)S(1)}, u32[]{:S(2)}, u32[]{:S(2)}) %all-to-all-start.6) | async-done | bytes 1048608 | tf_op jit(solution)/shard_map/all_to_all | solution.py:483
  266.7 3.6 %all-to-all-start.5 = ((bf16[8,64,1024]{2,1,0:T(8,128)(2,1)}), bf16[8,64,1024]{2,1,0:T(8,128)(2,1)S(1)}, u32[]{:S(2)}, u32[]{:S(2)}) async-start(bf16[8,64,1024]{2,1,0:T(8,128)(2,1)} %bitcast.22), calls=%async_computation.7 | async-start | bytes 2097152 | tf_op jit(solution)/shard_map/all_to_all | solution.py:483
  270.3 1.7 convolution_convert_fusion.2
  272.0 24.8 %all-to-all-done.5 = bf16[8,64,1024]{2,1,0:T(8,128)(2,1)S(1)} async-done(((bf16[8,64,1024]{2,1,0:T(8,128)(2,1)}), bf16[8,64,1024]{2,1,0:T(8,128)(2,1)S(1)}, u32[]{:S(2)}, u32[]{:S(2)}) %all-to-all-start.5) | async-done | bytes 1048608 | tf_op jit(solution)/shard_map/all_to_all | solution.py:483
  296.7 1.7 convolution_convert_fusion.4
  298.4 1.5 fusion.2
  299.9 8.2 %psum.15 = f32[512]{0:T(512)S(1)} all-reduce(f32[512]{0:T(512)S(1)} %fusion.2), channel_id=1, replica_groups=mesh['tok'=8,'rep'=4] {'rep'}, use_global_device_ids=true, to_apply=%region_14.15 | all-reduce | flops 512 | bytes 4096 | tf_op jit(solution)/shard_map/psum | solution.py:544
  308.2 3.3 %fusion.5 = bf16[512,1024]{1,0:T(8,128)(2,1)} fusion(bf16[512,1024]{1,0:T(8,128)(2,1)} %bitcast.11, f32[1024]{0:T(1024)S(1)} %copy-done.23, f32[512]{0:T(512)S(1)} %add_rsqrt_fusion.1, bf16[256,1024]{1,0:T(8,128)(2,1)} %bitcast.71, bf16[256,1024]{1,0:T(8,128)(2,1)} %bitcast.69, s32[512]{0:T(512)S(1)} %bitcast.75), kind=kOutput, calls=%fused_computation.15 | convolution fusion | flops 542375936 | bytes 3153920 | tf_op jit(solution)/shard_map/dot_general | solution.py:195
  (108 shorter events, 23.2 us)
Async XLA Ops:
  7.2 1.2 copy-start
  8.4 11.1 %copy-start.21 = (s32[4096]{0:T(1024)S(1)}, s32[4096]{0:T(1024)}, u32[]{:S(2)}) copy-start(s32[4096]{0:T(1024)} %param.24) | copy-start | bytes 49156
  8.4 11.6 %copy-start.24 = (s32[8]{0:T(128)S(1)}, s32[8]{0:T(128)}, u32[]{:S(2)}) copy-start(s32[8]{0:T(128)} %param.21) | copy-start | bytes 100
  10.1 33.8 %collective-permute-start.2 = (bf16[512,1024]{1,0:T(8,128)(2,1)}, bf16[512,1024]{1,0:T(8,128)(2,1)}, u32[]{:S(2)}, u32[]{:S(2)}) collective-permute-start(bf16[512,1024]{1,0:T(8,128)(2,1)} %convolution_convert_fusion.7), channel_id=1, source_target_pairs={{0,1},{1,0},{2,3},{3,2},{4,5},{5,4},{6,7},{7,6},{8,9},{9,8},{10,11... | collective-permute-start | bytes 3145736 | tf_op jit(solution)/shard_map/ppermute | solution.py:439
  13.1 30.2 %collective-permute-start = (bf16[512,1024]{1,0:T(8,128)(2,1)}, bf16[512,1024]{1,0:T(8,128)(2,1)S(1)}, u32[]{:S(2)}, u32[]{:S(2)}) collective-permute-start(bf16[512,1024]{1,0:T(8,128)(2,1)} %convolution_convert_fusion.7), channel_id=1, source_target_pairs={{0,2},{1,3},{2,0},{3,1},{4,6},{5,7},{6,4},{7,5},{8,10},{9,11},{10,... | collective-permute-start | bytes 3145736 | tf_op jit(solution)/shard_map/ppermute | solution.py:440
  14.6 48.1 %all-to-all-start = ((bf16[8,64,1024]{2,1,0:T(8,128)(2,1)}), bf16[8,64,1024]{2,1,0:T(8,128)(2,1)}, u32[]{:S(2)}, u32[]{:S(2)}) async-start(bf16[8,64,1024]{2,1,0:T(8,128)(2,1)} %bitcast), calls=%async_computation | async-start | bytes 2097152 | tf_op jit(solution)/shard_map/all_to_all | solution.py:460
  24.9 5.0 %copy-start.22 = (s32[4096]{0:T(1024)S(1)}, s32[4096]{0:T(1024)}, u32[]{:S(2)}) copy-start(s32[4096]{0:T(1024)} %param.23) | copy-start | bytes 49156
  36.1 13.0 %slice-start.2 = ((s8[8388608]{0:T(1024)(128)(4,1)}), s8[4194304]{0:T(1024)(128)(4,1)S(1)}, s32[]{:S(2)}) async-start(s8[8388608]{0:T(1024)(128)(4,1)} %bitcast.66), calls=%async_computation.13 | async-start | bytes 8388608
  43.3 5.8 %slice-start.3 = ((s8[8388608]{0:T(1024)(128)(4,1)}), s8[4194304]{0:T(1024)(128)(4,1)S(1)}, s32[]{:S(2)}) async-start(s8[8388608]{0:T(1024)(128)(4,1)} %bitcast.66), calls=%async_computation.14 | async-start | bytes 8388608
  43.3 19.3 %collective-permute-start.1 = (bf16[256,1024]{1,0:T(8,128)(2,1)S(1)}, bf16[256,1024]{1,0:T(8,128)(2,1)S(1)}, u32[]{:S(2)}, u32[]{:S(2)}) collective-permute-start(bf16[256,1024]{1,0:T(8,128)(2,1)S(1)} %slice.16), channel_id=1, source_target_pairs={{0,1},{1,0},{2,3},{3,2},{4,5},{5,4},{6,7},{7,6},{8,9},{9,8},{10,11... | collective-permute-start | bytes 1572872 | tf_op jit(solution)/shard_map/ppermute | solution.py:443
  45.3 17.3 %collective-permute-start.3 = (bf16[256,1024]{1,0:T(8,128)(2,1)S(1)}, bf16[256,1024]{1,0:T(8,128)(2,1)S(1)}, u32[]{:S(2)}, u32[]{:S(2)}) collective-permute-start(bf16[256,1024]{1,0:T(8,128)(2,1)S(1)} %slice.17), channel_id=1, source_target_pairs={{0,2},{1,3},{2,0},{3,1},{4,6},{5,7},{6,4},{7,5},{8,10},{9,11},{10,... | collective-permute-start | bytes 1572872 | tf_op jit(solution)/shard_map/ppermute | solution.py:444
  49.1 2.7 copy-start.20
  51.8 7.1 %slice-start = ((s8[8388608]{0:T(1024)(128)(4,1)}), s8[4194304]{0:T(1024)(128)(4,1)S(1)}, s32[]{:S(2)}) async-start(s8[8388608]{0:T(1024)(128)(4,1)} %bitcast.57), calls=%async_computation.11 | async-start | bytes 8388608
  56.2 2.7 slice-start.1
  62.7 3.4 %copy-start.2 = (bf16[4096,1024]{1,0:T(8,128)(2,1)S(1)}, bf16[4096,1024]{1,0:T(8,128)(2,1)}, u32[]{:S(2)}) copy-start(bf16[4096,1024]{1,0:T(8,128)(2,1)} %w_ref.1) | copy-start | bytes 25165828
  68.5 1.0 copy-start.14
  69.5 1.0 copy-start.8
  70.5 34.9 %all-to-all-start.2 = ((bf16[8,512,128]{2,1,0:T(8,128)(2,1)}), bf16[8,512,128]{2,1,0:T(8,128)(2,1)}, u32[]{:S(2)}, u32[]{:S(2)}) async-start(bf16[8,512,128]{2,1,0:T(8,128)(2,1)} %copy-done.8), calls=%async_computation.2 | async-start | bytes 2097152 | tf_op jit(solution)/shard_map/all_to_all | solution.py:483
  78.4 3.0 copy-start.19
  81.4 1.6 copy-start.18
  83.0 12.9 %copy-start.12 = (f32[1024]{0:T(1024)S(1)}, f32[1024]{0:T(1024)}, u32[]{:S(2)}) copy-start(f32[1024]{0:T(1024)} %param.18) | copy-start | bytes 12292
  83.0 12.9 %copy-start.13 = (f32[1024]{0:T(1024)S(1)}, f32[1024]{0:T(1024)}, u32[]{:S(2)}) copy-start(f32[1024]{0:T(1024)} %param.19) | copy-start | bytes 12292
  95.9 1.6 copy-start.3
  97.5 0.9 copy-start.5
  98.5 0.9 copy-start.6
  99.4 0.9 copy-start.7
  104.1 1.3 copy-start.4
  105.4 1.0 copy-start.16
  106.4 54.1 %all-to-all-start.1 = ((bf16[8,512,256]{2,1,0:T(8,128)(2,1)}), bf16[8,512,256]{2,1,0:T(8,128)(2,1)S(1)}, u32[]{:S(2)}, u32[]{:S(2)}) async-start(bf16[8,512,256]{2,1,0:T(8,128)(2,1)} %copy-done.4), calls=%async_computation.1 | async-start | bytes 4194304 | tf_op jit(solution)/shard_map/all_to_all | solution.py:483
  176.2 0.8 copy-start.11
  179.0 19.5 %all-to-all-start.3 = ((bf16[8,256,128]{1,2,0:T(8,128)(2,1)}), bf16[8,256,128]{1,2,0:T(8,128)(2,1)}, u32[]{:S(2)}, u32[]{:S(2)}) async-start(bf16[8,256,128]{1,2,0:T(8,128)(2,1)} %copy.21), calls=%async_computation.3 | async-start | bytes 1048576 | tf_op jit(solution)/shard_map/all_to_all | solution.py:483
  183.2 115.2 %reduce-scatter.3.cloned.1.call-start = ((), (), s32[]{:S(2)}) async-start(), calls=%async_computation.9 | async-start | bytes 2621440 | tf_op jit(solution)/shard_map/reduce_scatter | solution.py:524
  196.1 0.8 copy-start.9
  205.8 1.0 copy-start.10
  207.9 18.8 %all-to-all-start.4 = ((bf16[8,256,128]{1,2,0:T(8,128)(2,1)}), bf16[8,256,128]{1,2,0:T(8,128)(2,1)S(1)}, u32[]{:S(2)}, u32[]{:S(2)}) async-start(bf16[8,256,128]{1,2,0:T(8,128)(2,1)} %copy.22), calls=%async_computation.5 | async-start | bytes 1048576 | tf_op jit(solution)/shard_map/all_to_all | solution.py:483
  211.4 87.1 %reduce-scatter.5.cloned.1.call-start = ((), (), s32[]{:S(2)}) async-start(), calls=%async_computation.10 | async-start | bytes 2621440 | tf_op jit(solution)/shard_map/reduce_scatter | solution.py:524
  233.7 1.2 copy-start.15
  234.9 5.3 %copy-start.17 = (bf16[512,1024]{1,0:T(8,128)(2,1)S(1)}, bf16[512,1024]{1,0:T(8,128)(2,1)}, u32[]{:S(2)}) copy-start(bf16[512,1024]{1,0:T(8,128)(2,1)} %copy-done.16) | copy-start | bytes 3145732
  236.6 30.1 %all-to-all-start.6 = ((bf16[8,64,1024]{2,1,0:T(8,128)(2,1)}), bf16[8,64,1024]{2,1,0:T(8,128)(2,1)S(1)}, u32[]{:S(2)}, u32[]{:S(2)}) async-start(bf16[8,64,1024]{2,1,0:T(8,128)(2,1)} %bitcast.24), calls=%async_computation.8 | async-start | bytes 2097152 | tf_op jit(solution)/shard_map/all_to_all | solution.py:483
  266.7 30.1 %all-to-all-start.5 = ((bf16[8,64,1024]{2,1,0:T(8,128)(2,1)}), bf16[8,64,1024]{2,1,0:T(8,128)(2,1)S(1)}, u32[]{:S(2)}, u32[]{:S(2)}) async-start(bf16[8,64,1024]{2,1,0:T(8,128)(2,1)} %bitcast.22), calls=%async_computation.7 | async-start | bytes 2097152 | tf_op jit(solution)/shard_map/all_to_all | solution.py:483
  272.0 36.2 %copy-start.23 = (f32[1024]{0:T(1024)S(1)}, f32[1024]{0:T(1024)}, u32[]{:S(2)}) copy-start(f32[1024]{0:T(1024)} %param.20) | copy-start | bytes 12292
  308.2 3.3 %copy-start.1 = (bf16[512,1024]{1,0:T(8,128)(2,1)S(1)}, bf16[512,1024]{1,0:T(8,128)(2,1)}, u32[]{:S(2)}) copy-start(bf16[512,1024]{1,0:T(8,128)(2,1)} %param.13) | copy-start | bytes 3145732
Sparse Core Ops, SparseCore 0:
  206.0 33.2 reduce-scatter.2
  242.2 35.1 reduce-scatter.4

commit v4 on v3

--- a/solution.py
+++ b/solution.py
@@ -531,12 +531,9 @@
             )
         )
     cache_hits = slot_target[None, :] == local[:, None]
-    cache_keys, cache_values = [
-        select_rows(
-            cache_hits,
-            exchange(select_rows(slot_hits, rows).reshape(shards, chunk, width_dev)).reshape(
-                tok_rows, width_dev
-            ),
+    sent_keys, sent_values = [
+        exchange(select_rows(slot_hits, rows).reshape(shards, chunk, width_dev)).reshape(
+            tok_rows, width_dev
         )
         for rows in (key_flat, value_half)
     ]
@@ -546,6 +543,9 @@
         mixed_rows * lax.rsqrt(mixed_sums / full_width + EPSILON)[:, None] * post_gain[None, :]
     )
     output = (packed_hidden.astype(jnp.float32) + normed_rows).astype(jnp.bfloat16)
+    output, sent_keys = lax.optimization_barrier((output, sent_keys))
+    cache_keys = select_rows(cache_hits, sent_keys)
+    cache_values = select_rows(cache_hits, sent_values)
     return (output, cache_keys, cache_values)
 
 

time: 318 us -> 308 us (0.969)
  waiting for transfers between devices: 115 us -> 84.9 us
  blocking collectives: 17.8 us -> 38.6 us
  starting transfers between devices: 35.6 us -> 32.1 us
    all_to_all x6 -> x5, waiting for transfers between devices: 115 us -> 78.3 us  [exchange(): return lax.all_to_all(rows, 'tok', split_axis=0, concat_axis=0, tiled=True)]
    all_to_all x0 -> x1, blocking collectives: none -> 20.1 us  [exchange(): return lax.all_to_all(rows, 'tok', split_axis=0, concat_axis=0, tiled=True)]
    reduce_scatter x2, waiting for transfers between devices: 0.01 us -> 6.56 us  [body_heads(): lax.psum_scatter(lax.dot_general(w_out, rows, (((0,), (1,)), ((), ())), p...]
    all_to_all x6 -> x5, starting transfers between devices: 25 us -> 21.5 us  [exchange(): return lax.all_to_all(rows, 'tok', split_axis=0, concat_axis=0, tiled=True)]
  transfers between devices with their start and end apart: 13 -> 12, of which waited for: 5 -> 4; matrix products, arithmetic and copies ran while one was open for 21% -> 22% of each run, Pallas kernels for 5% -> 6%
where the time goes in v4:
time: 308 us; the launch traced here: 307 us
  waiting for transfers between devices  84.9 us (28%)
  matrix products  59.5 us (19%)
  blocking collectives  38.6 us (13%)
  Pallas kernels  37.6 us (12%)
  starting transfers between devices  32.1 us (10%)
  local copies, waits for them, and re-layouts  23.4 us (8%)
  other arithmetic  16.5 us (5%)
  between operations  14.5 us (5%)
    all_to_all x5, waiting for transfers between devices, exchange(): return lax.all_to_all(rows, 'tok', split_axis=0, concat_axis=0, tiled=True)  78.3 us
    dot_general x11, matrix products, product(): return jnp.dot(rows, owned, preferred_element_type=jnp.float32)  33.4 us
    pallas_call x2, Pallas kernels, attend_head(): pl.pallas_call(functools.partial(attend_kernel, size=tok_rows, head_size=...  31.5 us
    all_to_all x5, starting transfers between devices, exchange(): return lax.all_to_all(rows, 'tok', split_axis=0, concat_axis=0, tiled=True)  21.5 us
    all_to_all x1, blocking collectives, exchange(): return lax.all_to_all(rows, 'tok', split_axis=0, concat_axis=0, tiled=True)  20.1 us
    unnamed x59, local copies, waits for them, and re-layouts  17 us
    dot_general x2, matrix products, body_heads(): lax.dot_general(w_out, rows, (((0,), (1,)), ((), ())), preferred_element_...  14.3 us
    dot_general x6, matrix products, select_rows(): jnp.dot(hits.astype(jnp.bfloat16), rows, preferred_element_type=jnp.float32)  11.8 us
  transfers between devices with their start and end apart: 12, of which 4 were waited for; matrix products, arithmetic and copies ran while one was open for 22% of the time, Pallas kernels for 6%

profile of v4, /device:TPU:0, one launch (start us, length us, event | category | flops | bytes accessed | tf_op | source)
XLA Modules:
  0.0 307.1 jit_solution(5467306977817414311)
XLA Ops:
  8.4 1.7 convolution_convert_fusion.7
  10.1 3.0 collective-permute-start.2
  13.1 1.5 collective-permute-start
  14.6 4.9 %all-to-all-start = ((bf16[8,64,1024]{2,1,0:T(8,128)(2,1)}), bf16[8,64,1024]{2,1,0:T(8,128)(2,1)}, u32[]{:S(2)}, u32[]{:S(2)}) async-start(bf16[8,64,1024]{2,1,0:T(8,128)(2,1)} %bitcast), calls=%async_computation | async-start | bytes 2097152 | tf_op jit(solution)/shard_map/all_to_all | solution.py:460
  20.3 4.5 %fusion.14 = f32[512,1024]{1,0:T(8,128)} fusion(bf16[512,1024]{1,0:T(8,128)(2,1)} %convolution_convert_fusion.7, bf16[4096,1024]{1,0:T(8,128)(2,1)} %param.15, s32[]{:T(128)S(6)} %select_n.75), kind=kOutput, calls=%fused_computation.27 | convolution fusion | flops 1073741824 | bytes 5242884 | tf_op jit(solution)/shard_map/dot_general | solution.py:451
  24.8 3.2 %fusion.20 = f32[512,1024]{1,0:T(8,128)S(1)} fusion(bf16[512,1024]{1,0:T(8,128)(2,1)} %convolution_convert_fusion.7, bf16[4096,1024]{1,0:T(8,128)(2,1)} %param.14, s32[]{:T(128)S(6)} %select_n.75), kind=kOutput, calls=%fused_computation.34 | convolution fusion | flops 1073741824 | bytes 5242884 | tf_op jit(solution)/shard_map/dot_general | solution.py:451
  28.1 1.6 convert_reduce_fusion
  29.8 2.3 convert_reduce_fusion.1
  32.1 1.9 fusion.40
  34.0 2.1 pad_maximum_fusion.2
  36.1 3.3 %fusion.26 = f32[512,1024]{1,0:T(8,128)S(1)} fusion(bf16[512,1024]{1,0:T(8,128)(2,1)} %convolution_convert_fusion.7, bf16[4096,1024]{1,0:T(8,128)(2,1)} %w_ref.1, s32[]{:T(128)S(6)} %select_n.75), kind=kOutput, calls=%fused_computation.41 | convolution fusion | flops 1073741824 | bytes 5242884 | tf_op jit(solution)/shard_map/dot_general | solution.py:451
  40.7 2.6 select_reduce_fusion
  43.9 1.4 slice.17
  45.9 3.2 %fusion.12 = f32[512,1024]{1,0:T(8,128)S(1)} fusion(bf16[512,1024]{1,0:T(8,128)(2,1)} %collective-permute-done.2, bf16[4096,1024]{1,0:T(8,128)(2,1)} %param.15, s32[]{:T(128)S(6)} %select_n.76), kind=kOutput, calls=%fused_computation.25 | convolution fusion | flops 1073741824 | bytes 5242884 | tf_op jit(solution)/shard_map/dot_general | solution.py:451
  49.1 2.6 fusion.18
  51.8 4.3 %add_add_fusion = f32[512,1024]{1,0:T(8,128)} fusion(f32[512,1024]{1,0:T(8,128)S(1)} %copy-done.20, f32[512,1024]{1,0:T(8,128)S(1)} %fusion.12, bf16[512,1024]{1,0:T(8,128)(2,1)S(1)} %collective-permute-done, bf16[4096,1024]{1,0:T(8,128)(2,1)} %param.15, s32[]{:T(128)S(6)} %select_n.77), kind=kOutput, calls=%fused_computation.24 | convolution fusion | flops 1074790400 | bytes 9437188 | tf_op jit(solution)/shard_map/dot_general | solution.py:451
  56.1 2.7 add_add_fusion.1
  58.8 2.5 fusion.24
  62.7 3.4 %copy-done.2 = bf16[4096,1024]{1,0:T(8,128)(2,1)S(1)} copy-done((bf16[4096,1024]{1,0:T(8,128)(2,1)S(1)}, bf16[4096,1024]{1,0:T(8,128)(2,1)}, u32[]{:S(2)}) %copy-start.2) | copy-done | bytes 8388632
  66.1 2.4 shard_map.139
  70.4 5.1 %all-to-all-start.2 = ((bf16[8,512,128]{2,1,0:T(8,128)(2,1)}), bf16[8,512,128]{2,1,0:T(8,128)(2,1)}, u32[]{:S(2)}, u32[]{:S(2)}) async-start(bf16[8,512,128]{2,1,0:T(8,128)(2,1)} %copy-done.8), calls=%async_computation.2 | async-start | bytes 2097152 | tf_op jit(solution)/shard_map/all_to_all | solution.py:483
  75.5 2.8 fusion.6
  78.4 3.0 fusion.8
  83.0 1.6 multiply_reduce_fusion.1
  84.6 9.6 %psum.14 = f32[2,512]{1,0:T(2,128)S(1)} all-reduce(f32[2,512]{1,0:T(2,128)S(1)} %pad_maximum_fusion.4), channel_id=1, replica_groups=mesh['tok'=8,'rep'=4] {'rep'}, use_global_device_ids=true, to_apply=%region_10.11 | all-reduce | flops 1024 | bytes 8192 | tf_op jit(solution)/shard_map/psum | solution.py:492
  95.9 1.6 copy-done.3
  100.3 3.7 %shard_map.140 = (bf16[8,512,256]{2,1,0:T(8,128)(2,1)S(1)}, bf16[512,1024]{1,0:T(8,128)(2,1)S(1)}) custom-call(f32[512,1024]{1,0:T(8,128)S(1)} %copy-done.3, f32[512,1024]{1,0:T(8,128)S(1)} %get-tuple-element.58.k_ref, f32[512,1]{1,0:T(8,128)S(1)} %copy-done.6, f32[512,1]{1,0:T(8,128)S(1)} %copy-done.7, f32[1,1024]{1,0:T(1,128)S(1)} %bitcast.61, ...), custom_call_target="tpu_custom_call" | custom-call | flops 7340032 | bytes 7340032 | tf_op jit(solution)/shard_map/pallas_call | solution.py:320
  106.3 5.1 %all-to-all-start.1 = ((bf16[8,512,256]{2,1,0:T(8,128)(2,1)}), bf16[8,512,256]{2,1,0:T(8,128)(2,1)S(1)}, u32[]{:S(2)}, u32[]{:S(2)}) async-start(bf16[8,512,256]{2,1,0:T(8,128)(2,1)} %copy-done.4), calls=%async_computation.1 | async-start | bytes 4194304 | tf_op jit(solution)/shard_map/all_to_all | solution.py:483
  111.4 49.0 %all-to-all-done.1.qk_ref = bf16[8,512,256]{2,1,0:T(8,128)(2,1)S(1)} async-done(((bf16[8,512,256]{2,1,0:T(8,128)(2,1)}), bf16[8,512,256]{2,1,0:T(8,128)(2,1)S(1)}, u32[]{:S(2)}, u32[]{:S(2)}) %all-to-all-start.1) | async-done | bytes 2097184 | tf_op jit(solution)/shard_map/all_to_all | solution.py:483
  160.4 15.7 %shard_map.141 = bf16[2048,128]{1,0:T(8,128)(2,1)S(1)} custom-call(s32[8]{0:T(128)S(1)} %bitcast_subtract_fusion.starts_ref, s32[8,1,512]{2,1,0:T(1,128)S(1)} %broadcast_in_dim.110.target_ref, bf16[8,512,256]{2,1,0:T(8,128)(2,1)S(1)} %all-to-all-done.1.qk_ref, bf16[8,512,128]{2,1,0:T(8,128)(2,1)} %all-to-all-done.2.v_ref), custom_call_target="tpu_custom_call" | custom-call | flops 3221225472 | bytes 4194304 | tf_op jit(solution)/shard_map/pallas_call | solution.py:268
  176.9 2.1 copy.21
  179.0 4.1 %all-to-all-start.3 = ((bf16[8,256,128]{1,2,0:T(8,128)(2,1)}), bf16[8,256,128]{1,2,0:T(8,128)(2,1)}, u32[]{:S(2)}, u32[]{:S(2)}) async-start(bf16[8,256,128]{1,2,0:T(8,128)(2,1)} %copy.21), calls=%async_computation.3 | async-start | bytes 1048576 | tf_op jit(solution)/shard_map/all_to_all | solution.py:483
  183.2 15.8 %shard_map.142 = bf16[2048,128]{1,0:T(8,128)(2,1)S(1)} custom-call(s32[8]{0:T(128)S(1)} %bitcast_subtract_fusion.starts_ref, s32[8,1,512]{2,1,0:T(1,128)S(1)} %broadcast_in_dim.110.target_ref, bf16[8,512,256]{2,1,0:T(8,128)(2,1)S(1)} %all-to-all-done.1.qk_ref, bf16[8,512,128]{2,1,0:T(8,128)(2,1)} %all-to-all-done.2.v_ref), custom_call_target="tpu_custom_call" | custom-call | flops 3221225472 | bytes 4194304 | tf_op jit(solution)/shard_map/pallas_call | solution.py:268
  199.8 7.3 %fusion = bf16[4096,256]{0,1:T(8,128)(2,1)} fusion(bf16[256,1024]{0,1:T(8,128)(2,1)} %bitcast.15, bf16[1024,4096]{1,0:T(8,128)(2,1)} %param.17), kind=kOutput, calls=%fused_computation.8 | convolution fusion | flops 2148532224 | bytes 11010048 | tf_op jit(solution)/shard_map/dot_general | solution.py:525
  208.4 20.1 %all_to_all.35 = bf16[8,256,128]{1,2,0:T(8,128)(2,1)S(1)} all-to-all(bf16[8,256,128]{1,2,0:T(8,128)(2,1)S(1)} %copy.22), channel_id=1, replica_groups=mesh['tok'=8,'rep'=4] {'tok'}, dimensions={0} | all-to-all | bytes 1048576 | tf_op jit(solution)/shard_map/all_to_all | solution.py:483
  228.4 7.1 %fusion.1 = bf16[4096,256]{0,1:T(8,128)(2,1)} fusion(bf16[256,1024]{0,1:T(8,128)(2,1)S(1)} %bitcast.63, bf16[1024,4096]{1,0:T(8,128)(2,1)} %param.17), kind=kOutput, calls=%fused_computation.9 | convolution fusion | flops 2148532224 | bytes 11010048 | tf_op jit(solution)/shard_map/dot_general | solution.py:525
  236.7 1.7 convolution_convert_fusion.3
  238.4 3.6 %all-to-all-start.6 = ((bf16[8,64,1024]{2,1,0:T(8,128)(2,1)}), bf16[8,64,1024]{2,1,0:T(8,128)(2,1)S(1)}, u32[]{:S(2)}, u32[]{:S(2)}) async-start(bf16[8,64,1024]{2,1,0:T(8,128)(2,1)} %bitcast.24), calls=%async_computation.8 | async-start | bytes 2097152 | tf_op jit(solution)/shard_map/all_to_all | solution.py:483
  242.0 1.7 convolution_convert_fusion.5
  243.7 24.8 %all-to-all-done.6 = bf16[8,64,1024]{2,1,0:T(8,128)(2,1)S(1)} async-done(((bf16[8,64,1024]{2,1,0:T(8,128)(2,1)}), bf16[8,64,1024]{2,1,0:T(8,128)(2,1)S(1)}, u32[]{:S(2)}, u32[]{:S(2)}) %all-to-all-start.6) | async-done | bytes 1048608 | tf_op jit(solution)/shard_map/all_to_all | solution.py:483
  268.5 3.6 %all-to-all-start.5 = ((bf16[8,64,1024]{2,1,0:T(8,128)(2,1)}), bf16[8,64,1024]{2,1,0:T(8,128)(2,1)S(1)}, u32[]{:S(2)}, u32[]{:S(2)}) async-start(bf16[8,64,1024]{2,1,0:T(8,128)(2,1)} %bitcast.22), calls=%async_computation.7 | async-start | bytes 2097152 | tf_op jit(solution)/shard_map/all_to_all | solution.py:483
  272.1 1.7 convolution_convert_fusion.2
  273.8 6.6 %reduce-scatter.5.cloned.1.call-done = bf16[1024,256]{0,1:T(8,128)(2,1)} async-done(((bf16[4096,256]{0,1:T(8,128)(2,1)}), bf16[1024,256]{0,1:T(8,128)(2,1)}) %reduce-scatter.5.cloned.1.call-update) | async-done | bytes 524304 | tf_op jit(solution)/shard_map/reduce_scatter | solution.py:524
  280.3 1.5 fusion.2
  281.8 8.9 %psum.15 = f32[512]{0:T(512)S(1)} all-reduce(f32[512]{0:T(512)S(1)} %fusion.2), channel_id=1, replica_groups=mesh['tok'=8,'rep'=4] {'rep'}, use_global_device_ids=true, to_apply=%region_14.15 | all-reduce | flops 512 | bytes 4096 | tf_op jit(solution)/shard_map/psum | solution.py:541
  290.8 3.3 %fusion.5 = bf16[512,1024]{1,0:T(8,128)(2,1)} fusion(bf16[512,1024]{1,0:T(8,128)(2,1)} %bitcast.11, f32[1024]{0:T(1024)S(1)} %copy-done.23, f32[512]{0:T(512)S(1)} %add_rsqrt_fusion.1, bf16[256,1024]{1,0:T(8,128)(2,1)} %bitcast.71, bf16[256,1024]{1,0:T(8,128)(2,1)} %bitcast.69, s32[512]{0:T(512)S(1)} %bitcast.75), kind=kOutput, calls=%fused_computation.15 | convolution fusion | flops 542375936 | bytes 3153920 | tf_op jit(solution)/shard_map/dot_general | solution.py:195
  294.1 4.5 %all-to-all-done.5 = bf16[8,64,1024]{2,1,0:T(8,128)(2,1)S(1)} async-done(((bf16[8,64,1024]{2,1,0:T(8,128)(2,1)}), bf16[8,64,1024]{2,1,0:T(8,128)(2,1)S(1)}, u32[]{:S(2)}, u32[]{:S(2)}) %all-to-all-start.5) | async-done | bytes 1048608 | tf_op jit(solution)/shard_map/all_to_all | solution.py:483
  298.5 1.7 convolution_convert_fusion.4
  (107 shorter events, 20.6 us)
Async XLA Ops:
  7.2 1.2 copy-start
  8.4 11.1 %copy-start.21 = (s32[4096]{0:T(1024)S(1)}, s32[4096]{0:T(1024)}, u32[]{:S(2)}) copy-start(s32[4096]{0:T(1024)} %param.24) | copy-start | bytes 49156
  8.4 11.6 %copy-start.24 = (s32[8]{0:T(128)S(1)}, s32[8]{0:T(128)}, u32[]{:S(2)}) copy-start(s32[8]{0:T(128)} %param.21) | copy-start | bytes 100
  10.1 33.8 %collective-permute-start.2 = (bf16[512,1024]{1,0:T(8,128)(2,1)}, bf16[512,1024]{1,0:T(8,128)(2,1)}, u32[]{:S(2)}, u32[]{:S(2)}) collective-permute-start(bf16[512,1024]{1,0:T(8,128)(2,1)} %convolution_convert_fusion.7), channel_id=1, source_target_pairs={{0,1},{1,0},{2,3},{3,2},{4,5},{5,4},{6,7},{7,6},{8,9},{9,8},{10,11... | collective-permute-start | bytes 3145736 | tf_op jit(solution)/shard_map/ppermute | solution.py:439
  13.1 30.2 %collective-permute-start = (bf16[512,1024]{1,0:T(8,128)(2,1)}, bf16[512,1024]{1,0:T(8,128)(2,1)S(1)}, u32[]{:S(2)}, u32[]{:S(2)}) collective-permute-start(bf16[512,1024]{1,0:T(8,128)(2,1)} %convolution_convert_fusion.7), channel_id=1, source_target_pairs={{0,2},{1,3},{2,0},{3,1},{4,6},{5,7},{6,4},{7,5},{8,10},{9,11},{10,... | collective-permute-start | bytes 3145736 | tf_op jit(solution)/shard_map/ppermute | solution.py:440
  14.6 48.1 %all-to-all-start = ((bf16[8,64,1024]{2,1,0:T(8,128)(2,1)}), bf16[8,64,1024]{2,1,0:T(8,128)(2,1)}, u32[]{:S(2)}, u32[]{:S(2)}) async-start(bf16[8,64,1024]{2,1,0:T(8,128)(2,1)} %bitcast), calls=%async_computation | async-start | bytes 2097152 | tf_op jit(solution)/shard_map/all_to_all | solution.py:460
  24.8 5.0 %copy-start.22 = (s32[4096]{0:T(1024)S(1)}, s32[4096]{0:T(1024)}, u32[]{:S(2)}) copy-start(s32[4096]{0:T(1024)} %param.23) | copy-start | bytes 49156
  36.1 13.0 %slice-start.2 = ((s8[8388608]{0:T(1024)(128)(4,1)}), s8[4194304]{0:T(1024)(128)(4,1)S(1)}, s32[]{:S(2)}) async-start(s8[8388608]{0:T(1024)(128)(4,1)} %bitcast.66), calls=%async_computation.13 | async-start | bytes 8388608
  43.3 5.8 %slice-start.3 = ((s8[8388608]{0:T(1024)(128)(4,1)}), s8[4194304]{0:T(1024)(128)(4,1)S(1)}, s32[]{:S(2)}) async-start(s8[8388608]{0:T(1024)(128)(4,1)} %bitcast.66), calls=%async_computation.14 | async-start | bytes 8388608
  43.3 19.3 %collective-permute-start.1 = (bf16[256,1024]{1,0:T(8,128)(2,1)S(1)}, bf16[256,1024]{1,0:T(8,128)(2,1)S(1)}, u32[]{:S(2)}, u32[]{:S(2)}) collective-permute-start(bf16[256,1024]{1,0:T(8,128)(2,1)S(1)} %slice.16), channel_id=1, source_target_pairs={{0,1},{1,0},{2,3},{3,2},{4,5},{5,4},{6,7},{7,6},{8,9},{9,8},{10,11... | collective-permute-start | bytes 1572872 | tf_op jit(solution)/shard_map/ppermute | solution.py:443
  45.3 17.3 %collective-permute-start.3 = (bf16[256,1024]{1,0:T(8,128)(2,1)S(1)}, bf16[256,1024]{1,0:T(8,128)(2,1)S(1)}, u32[]{:S(2)}, u32[]{:S(2)}) collective-permute-start(bf16[256,1024]{1,0:T(8,128)(2,1)S(1)} %slice.17), channel_id=1, source_target_pairs={{0,2},{1,3},{2,0},{3,1},{4,6},{5,7},{6,4},{7,5},{8,10},{9,11},{10,... | collective-permute-start | bytes 1572872 | tf_op jit(solution)/shard_map/ppermute | solution.py:444
  49.1 2.7 copy-start.20
  51.8 7.0 %slice-start = ((s8[8388608]{0:T(1024)(128)(4,1)}), s8[4194304]{0:T(1024)(128)(4,1)S(1)}, s32[]{:S(2)}) async-start(s8[8388608]{0:T(1024)(128)(4,1)} %bitcast.57), calls=%async_computation.11 | async-start | bytes 8388608
  56.1 2.7 slice-start.1
  62.7 3.4 %copy-start.2 = (bf16[4096,1024]{1,0:T(8,128)(2,1)S(1)}, bf16[4096,1024]{1,0:T(8,128)(2,1)}, u32[]{:S(2)}) copy-start(bf16[4096,1024]{1,0:T(8,128)(2,1)} %w_ref.1) | copy-start | bytes 25165828
  68.5 1.0 copy-start.14
  69.5 1.0 copy-start.8
  70.4 34.9 %all-to-all-start.2 = ((bf16[8,512,128]{2,1,0:T(8,128)(2,1)}), bf16[8,512,128]{2,1,0:T(8,128)(2,1)}, u32[]{:S(2)}, u32[]{:S(2)}) async-start(bf16[8,512,128]{2,1,0:T(8,128)(2,1)} %copy-done.8), calls=%async_computation.2 | async-start | bytes 2097152 | tf_op jit(solution)/shard_map/all_to_all | solution.py:483
  78.4 3.0 copy-start.19
  81.4 1.6 copy-start.18
  83.0 12.9 %copy-start.12 = (f32[1024]{0:T(1024)S(1)}, f32[1024]{0:T(1024)}, u32[]{:S(2)}) copy-start(f32[1024]{0:T(1024)} %param.18) | copy-start | bytes 12292
  83.0 12.9 %copy-start.13 = (f32[1024]{0:T(1024)S(1)}, f32[1024]{0:T(1024)}, u32[]{:S(2)}) copy-start(f32[1024]{0:T(1024)} %param.19) | copy-start | bytes 12292
  95.9 1.6 copy-start.3
  97.5 0.9 copy-start.5
  98.4 0.9 copy-start.6
  99.4 0.9 copy-start.7
  104.0 1.3 copy-start.4
  105.3 1.0 copy-start.16
  106.3 54.1 %all-to-all-start.1 = ((bf16[8,512,256]{2,1,0:T(8,128)(2,1)}), bf16[8,512,256]{2,1,0:T(8,128)(2,1)S(1)}, u32[]{:S(2)}, u32[]{:S(2)}) async-start(bf16[8,512,256]{2,1,0:T(8,128)(2,1)} %copy-done.4), calls=%async_computation.1 | async-start | bytes 4194304 | tf_op jit(solution)/shard_map/all_to_all | solution.py:483
  176.1 0.8 copy-start.11
  179.0 20.8 %all-to-all-start.3 = ((bf16[8,256,128]{1,2,0:T(8,128)(2,1)}), bf16[8,256,128]{1,2,0:T(8,128)(2,1)}, u32[]{:S(2)}, u32[]{:S(2)}) async-start(bf16[8,256,128]{1,2,0:T(8,128)(2,1)} %copy.21), calls=%async_computation.3 | async-start | bytes 1048576 | tf_op jit(solution)/shard_map/all_to_all | solution.py:483
  183.1 90.6 %reduce-scatter.3.cloned.1.call-start = ((), (), s32[]{:S(2)}) async-start(), calls=%async_computation.9 | async-start | bytes 2621440 | tf_op jit(solution)/shard_map/reduce_scatter | solution.py:524
  199.0 0.8 copy-start.9
  207.1 1.0 copy-start.10
  207.1 73.2 %reduce-scatter.5.cloned.1.call-start = ((), (), s32[]{:S(2)}) async-start(), calls=%async_computation.10 | async-start | bytes 2621440 | tf_op jit(solution)/shard_map/reduce_scatter | solution.py:524
  235.5 1.2 copy-start.15
  236.7 5.3 %copy-start.17 = (bf16[512,1024]{1,0:T(8,128)(2,1)S(1)}, bf16[512,1024]{1,0:T(8,128)(2,1)}, u32[]{:S(2)}) copy-start(bf16[512,1024]{1,0:T(8,128)(2,1)} %copy-done.16) | copy-start | bytes 3145732
  238.4 30.1 %all-to-all-start.6 = ((bf16[8,64,1024]{2,1,0:T(8,128)(2,1)}), bf16[8,64,1024]{2,1,0:T(8,128)(2,1)S(1)}, u32[]{:S(2)}, u32[]{:S(2)}) async-start(bf16[8,64,1024]{2,1,0:T(8,128)(2,1)} %bitcast.24), calls=%async_computation.8 | async-start | bytes 2097152 | tf_op jit(solution)/shard_map/all_to_all | solution.py:483
  268.5 30.1 %all-to-all-start.5 = ((bf16[8,64,1024]{2,1,0:T(8,128)(2,1)}), bf16[8,64,1024]{2,1,0:T(8,128)(2,1)S(1)}, u32[]{:S(2)}, u32[]{:S(2)}) async-start(bf16[8,64,1024]{2,1,0:T(8,128)(2,1)} %bitcast.22), calls=%async_computation.7 | async-start | bytes 2097152 | tf_op jit(solution)/shard_map/all_to_all | solution.py:483
  272.1 18.7 %copy-start.23 = (f32[1024]{0:T(1024)S(1)}, f32[1024]{0:T(1024)}, u32[]{:S(2)}) copy-start(f32[1024]{0:T(1024)} %param.20) | copy-start | bytes 12292
  290.8 9.5 %copy-start.1 = (bf16[512,1024]{1,0:T(8,128)(2,1)S(1)}, bf16[512,1024]{1,0:T(8,128)(2,1)}, u32[]{:S(2)}) copy-start(bf16[512,1024]{1,0:T(8,128)(2,1)} %param.13) | copy-start | bytes 3145732
Sparse Core Ops, SparseCore 0:
  207.2 34.8 reduce-scatter.2
  245.1 35.1 reduce-scatter.4
